TPU v7x, 32 devices: a whole 2x2x4 slice. The times are simulated.
32 devices in a mesh: cx: 8 (over z, x), cy: 4 (over y, core).
Axes of the slice: x: 2, y: 2, z: 4, core: 2. Of those that a mesh axis runs over, the one named last changes fastest.
Arguments:
- cell_pos: float32 [32, 16, 3, 1024], P('cx', 'cy'), may hold values from -6 to 6
- cell_drag: float32 [32, 16], P('cx', 'cy'), may hold values from 0.2 to 2
- cell_near: int32 [32, 16, 2], P('cx', 'cy'), may hold values from 0 to 511, as said below
- analysis: bfloat16 [1024, 1024], replicated, may hold values from -0.1875 to 0.1875
- stiffness: float32 [1024], replicated, may hold values from 0.1 to 1
- synthesis: bfloat16 [1024, 1024], replicated, may hold values from -0.1875 to 0.1875
- wall_pos: float32 [256, 3, 256], P(('cx', 'cy')), may hold values from -9 to 9
- wall_normal: float32 [256, 3, 256], P(('cx', 'cy')), may hold values from -6 to 6
- wall_weight: float32 [256, 256], P(('cx', 'cy')), may hold values from 0.02 to 0.2
- density: float32 [256, 3, 256], P(('cx', 'cy')), may hold values from -6 to 6
- patch_near: int32 [256, 4], P(('cx', 'cy')), may hold values from 0 to 255, as said below
- cell_to_patch: int32 [256, 2], P(('cx', 'cy')), may hold values from 0 to 511, as said below
Outputs:
- moved_cells: float32 [32, 16, 3, 1024], P('cx', 'cy')
- density_next: float32 [256, 3, 256], P(('cx', 'cy'))
Inputs may be any that keep to these rules, and one draw needn't show every extreme that they name: `cell_near`: each entry is the row-major index (row times 16 plus column) of a cell whose grid row and column differ from the listing cell's by at most 3 each, cyclically, and never the listing cell itself. `cell_to_patch`: for the patches of block b (patches b * 8 to b * 8 + 7), with b = i * 4 + j, each entry is the row-major index of a cell whose row lies within 3 of the rows i * 4 to i * 4 + 3 and whose column lies within 3 of the columns j * 4 to j * 4 + 3, cyclically. `patch_near`: each entry is a patch of the listing patch's block of 8 or of the two blocks beside it, cyclically, and never the listing patch itself.
All inputs are finite; a program needn't handle non-finite values.
Results may differ from a plain program's by a relative error of at most 0.0041.
Values sent between devices are 32-bit elements; how exact they have to be, the bound alone decides.
A program may use at most 64 MiB of HBM per device.

v0:
```python
import math

import jax
import jax.numpy as jnp
from jax import lax
from jax.sharding import PartitionSpec as P

HALO = 3


soften = 0.25
stokes_scale = 1.0 / (8.0 * math.pi)
layer_scale = 3.0 / (4.0 * math.pi)


def with_halo(value, sides, width):
    for axis, dim in sides:
        size, length = (lax.axis_size(axis), value.shape[dim])
        up = [(i, (i + 1) % size) for i in range(size)]
        down = [(j, i) for i, j in up]
        last = lax.slice_in_dim(value, length - width, length, axis=dim)
        initial = lax.slice_in_dim(value, 0, width, axis=dim)
        before = lax.ppermute(last, axis, up)
        after = lax.ppermute(initial, axis, down)
        value = jnp.concatenate([before, value, after], axis=dim)
    return value


def membrane(positions, analysis, stiffness, synthesis):
    points = positions.shape[-1]
    centred = positions - jnp.mean(positions, axis=-1, keepdims=True)
    flat = centred.reshape(-1, points).astype(jnp.bfloat16)
    coeff = jnp.dot(flat, analysis, preferred_element_type=jnp.float32)
    scaled = (coeff * stiffness[None, :]).astype(jnp.bfloat16)
    force = -jnp.dot(scaled, synthesis, preferred_element_type=jnp.float32)
    return force.reshape(positions.shape)


def stokeslet(targets, sources, forces):
    delta_x = targets[0][:, None] - sources[0][None, :]
    delta_y = targets[1][:, None] - sources[1][None, :]
    delta_z = targets[2][:, None] - sources[2][None, :]
    square = delta_x * delta_x + delta_y * delta_y + delta_z * delta_z + soften
    factor = lax.rsqrt(square) / square
    along = (
        delta_x * forces[0][None, :] + delta_y * forces[1][None, :] + delta_z * forces[2][None, :]
    )
    direct = (square + soften) * factor
    tangent = along * factor
    out_x = jnp.sum(direct * forces[0][None, :] + tangent * delta_x, axis=1)
    out_y = jnp.sum(direct * forces[1][None, :] + tangent * delta_y, axis=1)
    out_z = jnp.sum(direct * forces[2][None, :] + tangent * delta_z, axis=1)
    return stokes_scale * jnp.stack([out_x, out_y, out_z])


def double_layer(targets, sources, normals, weights, values):
    delta_x = targets[0][:, None] - sources[0][None, :]
    delta_y = targets[1][:, None] - sources[1][None, :]
    delta_z = targets[2][:, None] - sources[2][None, :]
    square = delta_x * delta_x + delta_y * delta_y + delta_z * delta_z + soften
    factor = lax.rsqrt(square) / (square * square)
    along_q = (
        delta_x * values[0][None, :] + delta_y * values[1][None, :] + delta_z * values[2][None, :]
    )
    along_n = (
        delta_x * normals[0][None, :]
        + delta_y * normals[1][None, :]
        + delta_z * normals[2][None, :]
    )
    scalar = -layer_scale * weights[None, :] * along_q * along_n * factor
    return jnp.stack(
        [
            jnp.sum(scalar * delta_x, axis=1),
            jnp.sum(scalar * delta_y, axis=1),
            jnp.sum(scalar * delta_z, axis=1),
        ]
    )


def spread_many(picked):
    leading = picked.shape[:-3]
    count = picked.shape[-3]
    moved = jnp.swapaxes(picked, -3, -2)
    return moved.reshape(leading + (3, count * picked.shape[-1]))


def local_slot(global_id, first_row, first_col, all_rows, all_cols, ext_cols):
    grid_row = global_id // all_cols
    grid_col = global_id % all_cols
    local_row = (grid_row - first_row + HALO) % all_rows
    local_col = (grid_col - first_col + HALO) % all_cols
    return local_row * ext_cols + local_col


def body(
    cell_pos,
    cell_drag,
    cell_near,
    analysis,
    stiffness,
    synthesis,
    wall_pos,
    wall_normal,
    wall_weight,
    density,
    patch_near,
    cell_to_patch,
):
    row_count = cell_pos.shape[0]
    col_count = cell_pos.shape[1]
    points = cell_pos.shape[3]
    ext_pos = with_halo(cell_pos, (("cx", 0), ("cy", 1)), HALO)
    ext_force = membrane(ext_pos, analysis, stiffness, synthesis)
    own_force = ext_force[HALO : HALO + row_count, HALO : HALO + col_count]
    ext_cols = col_count + 2 * HALO
    flat_pos = ext_pos.reshape(-1, 3, points)
    flat_force = ext_force.reshape(-1, 3, points)
    all_rows = row_count * lax.axis_size("cx")
    all_cols = col_count * lax.axis_size("cy")
    first_row = lax.axis_index("cx") * row_count
    first_col = lax.axis_index("cy") * col_count
    near_slots = local_slot(cell_near, first_row, first_col, all_rows, all_cols, ext_cols)
    source_pos = spread_many(flat_pos[near_slots])
    source_force = spread_many(flat_force[near_slots])

    def one_row(pieces):
        return jax.vmap(stokeslet)(pieces[0], pieces[1], pieces[2])

    near = lax.map(one_row, (cell_pos, source_pos, source_force))
    velocity = cell_drag[:, :, None, None] * own_force + near
    speed = jnp.sqrt(jnp.sum(velocity * velocity, axis=2))
    top = lax.pmax(jnp.max(speed), ("cx", "cy"))
    step = 1.0 / (top + 1e-06)
    moved_cells = cell_pos + step * velocity
    patch_count = wall_pos.shape[0]
    wall_slots = local_slot(cell_to_patch, first_row, first_col, all_rows, all_cols, ext_cols)
    wall_source_pos = spread_many(flat_pos[wall_slots])
    wall_source_force = spread_many(flat_force[wall_slots])

    def wall_from_cells(pieces):
        return stokeslet(pieces[0], pieces[1], pieces[2])

    wall_velocity = lax.map(wall_from_cells, (wall_pos, wall_source_pos, wall_source_force))
    packed = jnp.concatenate([wall_pos, wall_normal, density, wall_weight[:, None, :]], axis=1)
    ext_wall = with_halo(packed, ((("cx", "cy"), 0),), patch_count)
    all_patches = patch_count * lax.axis_size(("cx", "cy"))
    block_start = lax.axis_index(("cx", "cy")) * patch_count
    own_slots = jnp.arange(patch_count, dtype=jnp.int32) + patch_count
    other_slots = (patch_near - block_start + patch_count) % all_patches
    chosen = jnp.concatenate([own_slots[:, None], other_slots], axis=1)
    gathered = ext_wall[chosen]
    listed = gathered.shape[1]
    merged = jnp.swapaxes(gathered, 1, 2).reshape(patch_count, 10, listed * gathered.shape[-1])

    def layer_patch(pieces):
        target, sources = pieces
        return double_layer(target, sources[0:3], sources[3:6], sources[9], sources[6:9])

    layer = lax.map(layer_patch, (wall_pos, merged))
    density_next = 2.0 * layer + 2.0 * wall_velocity
    return (moved_cells, density_next)


def solution(mesh):
    placed = (
        P("cx", "cy", None, None),
        P("cx", "cy"),
        P("cx", "cy", None),
        P(),
        P(),
        P(),
        P(("cx", "cy"), None, None),
        P(("cx", "cy"), None, None),
        P(("cx", "cy"), None),
        P(("cx", "cy"), None, None),
        P(("cx", "cy"), None),
        P(("cx", "cy"), None),
    )
    return jax.shard_map(
        body,
        mesh=mesh,
        in_specs=placed,
        out_specs=(P("cx", "cy", None, None), P(("cx", "cy"), None, None)),
        check_vma=False,
    )
```

profile of v0, /device:TPU:0, one launch (start us, length us, event | category | flops | bytes accessed | tf_op | source)
XLA Modules:
  0.0 331.3 jit_solution(6227901740022177289)
XLA Ops:
  3.8 6.5 %collective-permute-start.5 = (f32[8,10,256]{2,1,0:T(8,128)S(1)}, f32[8,10,256]{2,1,0:T(8,128)S(1)}, u32[]{:S(2)}, u32[]{:S(2)}) collective-permute-start(f32[8,10,256]{2,1,0:T(8,128)S(1)} %pad_maximum_fusion.2), channel_id=1, source_target_pairs={{1,0},{2,1},{3,2},{4,3},{5,4},{6,5},{7,6},{8,7},{9,8},{10,9},{11,1... | collective-permute-start | bytes 245768 | tf_op jit(solution)/shard_map/ppermute | solution.py:24
  24.0 2.8 collective-permute-start.3
  26.9 22.2 %while.35 = (s32[]{:T(128)}, f32[8,3,256]{2,0,1:T(8,128)S(1)}, f32[8,10,1280]{2,0,1:T(8,128)S(1)}, f32[8,3,256]{2,0,1:T(8,128)}, s32[]{:T(128)}, /*index=5*/s32[...) while((s32[]{:T(128)}, f32[8,3,256]{2,0,1:T(8,128)S(1)}, ...), condition=%wide.region_13.14_spmd, body=%wide.region_9.13_spmd.sunk | while | flops 9832459 | bytes 184633 | solution.py:159
  49.1 3.0 fusion.71
  52.4 3.6 %copy.100 = f32[10,10,3,1024]{3,2,1,0:T(4,128)} copy(f32[10,10,3,1024]{3,1,2,0:T(8,128)} %get-tuple-element.282) | data formatting | bytes 2457600 | tf_op jit(solution)/shard_map/concatenate | solution.py:25
  56.0 3.0 concatenate.52
  59.0 2.8 gather_fusion.3
  61.8 3.0 gather_fusion
  64.9 3.5 %convolution_negate_fusion = f32[300,1024]{1,0:T(8,128)S(1)} fusion(bf16[1024,1024]{1,0:T(8,128)(2,1)S(1)} %copy-done, bf16[1024,1024]{1,0:T(8,128)(2,1)} %param.21, f32[300,1024]{1,0:T(8,128)} %concatenate.52, f32[1024]{0:T(1024)S(1)} %copy-done.8, f32[300]{0:T(512)S(1)} %div.52), kind=kOutput, calls=%fused_computation.130 | convolution fusion | flops 1259827200 | bytes 6657200 | tf_op jit(solution)/shard_map/dot_general | solution.py:35
  70.1 2.8 gather_fusion.4
  72.9 3.1 gather_fusion.1
  87.7 164.7 %while.34 = (s32[]{:T(128)}, f32[4,4,3,1024]{3,1,2,0:T(4,128)}, f32[4,4,3,1024]{3,1,2,0:T(4,128)S(1)}, f32[4,4,3,2048]{3,1,2,0:T(4,128)S(1)}, f32[4,4,3,2048]{3,1,2,0:T(4,128)S(1)}, /*index=5*/s32[]{:T(128)}) while((s32[]{:T(128)}, f32[4,4,3,1024]{3,1,2,0:T(4,128)}, f32[4,4,3,1024]{3,1,2,0:T(4,128)S(1)}, f32[4,4,3,2048]{3,1,2,0:T(4,128)S(1)}, ...), condition=%wide.region_5.6_spmd, body=%wide.region_1.5_spmd.sunk | while | flops 251682816 | bytes 1376345 | solution.py:129
  87.9 40.4 %fusion.81 = (f32[4,1024]{1,0:T(4,128)S(1)}, f32[4,1024]{1,0:T(4,128)S(1)}, f32[4,1024]{1,0:T(4,128)S(1)}) fusion(f32[4,2048]{1,0:T(4,128)S(1)} %get-tuple-element.410, f32[4,2048]{1,0:T(4,128)S(1)} %get-tuple-element.412, f32[4,1024]{1,0:T(4,128)S(1)} %get-tuple-element.413, f32[4,2048]{1,0:T(4,128)S(1)} %get-tuple-element.414, ...), kind=kLoop, calls=%fused_computation.21.clone.1 | loop fusion | flops 251645952 | bytes 294912 | tf_op jit(solution)/shard_map/while/body/eval_jaxpr/vmap()/reduce_sum | solution.py:50
  129.1 40.4 %fusion.81 = (f32[4,1024]{1,0:T(4,128)S(1)}, f32[4,1024]{1,0:T(4,128)S(1)}, f32[4,1024]{1,0:T(4,128)S(1)}) fusion(f32[4,2048]{1,0:T(4,128)S(1)} %get-tuple-element.410, f32[4,2048]{1,0:T(4,128)S(1)} %get-tuple-element.412, f32[4,1024]{1,0:T(4,128)S(1)} %get-tuple-element.413, f32[4,2048]{1,0:T(4,128)S(1)} %get-tuple-element.414, ...), kind=kLoop, calls=%fused_computation.21.clone.1 | loop fusion | flops 251645952 | bytes 294912 | tf_op jit(solution)/shard_map/while/body/eval_jaxpr/vmap()/reduce_sum | solution.py:50
  170.2 40.4 %fusion.81 = (f32[4,1024]{1,0:T(4,128)S(1)}, f32[4,1024]{1,0:T(4,128)S(1)}, f32[4,1024]{1,0:T(4,128)S(1)}) fusion(f32[4,2048]{1,0:T(4,128)S(1)} %get-tuple-element.410, f32[4,2048]{1,0:T(4,128)S(1)} %get-tuple-element.412, f32[4,1024]{1,0:T(4,128)S(1)} %get-tuple-element.413, f32[4,2048]{1,0:T(4,128)S(1)} %get-tuple-element.414, ...), kind=kLoop, calls=%fused_computation.21.clone.1 | loop fusion | flops 251645952 | bytes 294912 | tf_op jit(solution)/shard_map/while/body/eval_jaxpr/vmap()/reduce_sum | solution.py:50
  211.3 40.4 %fusion.81 = (f32[4,1024]{1,0:T(4,128)S(1)}, f32[4,1024]{1,0:T(4,128)S(1)}, f32[4,1024]{1,0:T(4,128)S(1)}) fusion(f32[4,2048]{1,0:T(4,128)S(1)} %get-tuple-element.410, f32[4,2048]{1,0:T(4,128)S(1)} %get-tuple-element.412, f32[4,1024]{1,0:T(4,128)S(1)} %get-tuple-element.413, f32[4,2048]{1,0:T(4,128)S(1)} %get-tuple-element.414, ...), kind=kLoop, calls=%fused_computation.21.clone.1 | loop fusion | flops 251645952 | bytes 294912 | tf_op jit(solution)/shard_map/while/body/eval_jaxpr/vmap()/reduce_sum | solution.py:50
  255.2 36.3 %while.36 = (s32[]{:T(128)}, f32[8,3,256]{2,0,1:T(8,128)S(1)}, f32[8,3,256]{2,0,1:T(8,128)}, f32[8,3,2048]{2,0,1:T(8,128)}, f32[8,3,2048]{2,0,1:T(8,128)S(1)}, /*index=5*/s32[]{:T(128)}, s32[]{:T(128)}, s32[]{}, s32[]{}) while((s32[]{:T(128)}, f32[8,3,256]{2,0,1:T(8,128)S(1)}, f32[8,3,256]{2,0,1:T(8,128)}, f32[8,3,2048]{2,0,1:T(8,128)}, ...), condition=%wide.region_18.19_spmd, body=%wide.region_14.18_spmd.sunk | while | flops 15730180 | bytes 178329 | solution.py:143
  256.9 2.7 fusion.85
  261.4 2.7 fusion.85
  265.9 2.7 fusion.85
  279.6 2.7 fusion.85
  284.1 2.7 fusion.85
  288.6 2.7 fusion.85
  291.5 37.7 %pmax.7 = f32[]{:T(128)} all-reduce(f32[]{:T(128)} %sqrt_reduce_fusion), channel_id=1, replica_groups=mesh['cx'=8,'cy'=4] {'cx','cy'}, use_global_device_ids=true, to_apply=%region_8.9 | all-reduce | flops 1 | bytes 8 | tf_op jit(solution)/shard_map/pmax | solution.py:132
  (190 shorter events, 79.1 us)
Async XLA Ops:
  0.6 64.3 %copy-start = (bf16[1024,1024]{1,0:T(8,128)(2,1)S(1)}, bf16[1024,1024]{1,0:T(8,128)(2,1)}, u32[]{:S(2)}) copy-start(bf16[1024,1024]{1,0:T(8,128)(2,1)} %param.23) | copy-start | bytes 6291460
  3.8 12.9 %collective-permute-start.5 = (f32[8,10,256]{2,1,0:T(8,128)S(1)}, f32[8,10,256]{2,1,0:T(8,128)S(1)}, u32[]{:S(2)}, u32[]{:S(2)}) collective-permute-start(f32[8,10,256]{2,1,0:T(8,128)S(1)} %pad_maximum_fusion.2), channel_id=1, source_target_pairs={{1,0},{2,1},{3,2},{4,3},{5,4},{6,5},{7,6},{8,7},{9,8},{10,9},{11,1... | collective-permute-start | bytes 245768 | tf_op jit(solution)/shard_map/ppermute | solution.py:24
  10.3 8.0 %collective-permute-start.4 = (f32[8,10,256]{2,1,0:T(8,128)S(1)}, f32[8,10,256]{2,1,0:T(8,128)S(1)}, u32[]{:S(2)}, u32[]{:S(2)}) collective-permute-start(f32[8,10,256]{2,1,0:T(8,128)S(1)} %pad_maximum_fusion.2), channel_id=1, source_target_pairs={{0,1},{1,2},{2,3},{3,4},{4,5},{5,6},{6,7},{7,8},{8,9},{9,10},{10,1... | collective-permute-start | bytes 245768 | tf_op jit(solution)/shard_map/ppermute | solution.py:23
  12.0 10.8 %collective-permute-start.1 = (f32[3,4,3,1024]{3,1,2,0:T(4,128)}, f32[3,4,3,1024]{3,1,2,0:T(4,128)S(1)}, u32[]{:S(2)}, u32[]{:S(2)}) collective-permute-start(f32[3,4,3,1024]{3,1,2,0:T(4,128)} %get-tuple-element.285), channel_id=1, source_target_pairs={{4,0},{8,4},{12,8},{16,12},{20,16},{24,20},{28,24},{0,28},{5,1},{9... | collective-permute-start | bytes 442376 | tf_op jit(solution)/shard_map/ppermute | solution.py:24
  12.5 9.3 %collective-permute-start = (f32[3,4,3,1024]{3,1,2,0:T(4,128)}, f32[3,4,3,1024]{3,1,2,0:T(4,128)}, u32[]{:S(2)}, u32[]{:S(2)}) collective-permute-start(f32[3,4,3,1024]{3,1,2,0:T(4,128)} %get-tuple-element.286), channel_id=1, source_target_pairs={{0,4},{4,8},{8,12},{12,16},{16,20},{20,24},{24,28},{28,0},{1,5},{5... | collective-permute-start | bytes 442376 | tf_op jit(solution)/shard_map/ppermute | solution.py:23
  18.3 4.4 %copy-start.1 = (f32[4,4,3,1024]{3,1,2,0:T(4,128)S(1)}, f32[4,4,3,1024]{3,1,2,0:T(4,128)}, u32[]{:S(2)}) copy-start(f32[4,4,3,1024]{3,1,2,0:T(4,128)} %param.18) | copy-start | bytes 589828
  24.0 25.0 %collective-permute-start.2 = (f32[10,3,3,1024]{3,1,2,0:T(4,128)}, f32[10,3,3,1024]{3,1,2,0:T(4,128)}, u32[]{:S(2)}, u32[]{:S(2)}) collective-permute-start(f32[10,3,3,1024]{3,1,2,0:T(4,128)} %get-tuple-element.283), channel_id=1, source_target_pairs={{0,1},{1,2},{2,3},{3,0},{4,5},{5,6},{6,7},{7,4},{8,9},{9,10},{10,1... | collective-permute-start | bytes 1105928 | tf_op jit(solution)/shard_map/ppermute | solution.py:23
  24.0 25.0 %collective-permute-start.3 = (f32[10,3,3,1024]{3,1,2,0:T(4,128)}, f32[10,3,3,1024]{3,1,2,0:T(4,128)}, u32[]{:S(2)}, u32[]{:S(2)}) collective-permute-start(f32[10,3,3,1024]{3,1,2,0:T(4,128)} %get-tuple-element.284), channel_id=1, source_target_pairs={{1,0},{2,1},{3,2},{0,3},{5,4},{6,5},{7,6},{4,7},{9,8},{10,9},{11,1... | collective-permute-start | bytes 1105928 | tf_op jit(solution)/shard_map/ppermute | solution.py:24
  49.1 6.9 %copy-start.5 = (f32[8,3,256]{2,0,1:T(8,128)}, f32[8,3,256]{2,0,1:T(8,128)S(1)}, u32[]{:S(2)}) copy-start(f32[8,3,256]{2,0,1:T(8,128)S(1)} %get-tuple-element.155) | copy-start | bytes 73732
  56.0 8.9 %copy-start.8 = (f32[1024]{0:T(1024)S(1)}, f32[1024]{0:T(1024)}, u32[]{:S(2)}) copy-start(f32[1024]{0:T(1024)} %param.22) | copy-start | bytes 12292
  77.7 5.5 %copy-start.2 = (f32[32,3,1024]{2,1,0:T(4,128)S(1)}, f32[32,3,1024]{2,1,0:T(4,128)}, u32[]{:S(2)}) copy-start(f32[32,3,1024]{2,1,0:T(4,128)} %gather_fusion.1) | copy-start | bytes 1179652
  77.7 8.0 %copy-start.3 = (f32[16,3,1024]{2,1,0:T(4,128)S(1)}, f32[16,3,1024]{2,1,0:T(4,128)}, u32[]{:S(2)}) copy-start(f32[16,3,1024]{2,1,0:T(4,128)} %gather_fusion.4) | copy-start | bytes 589828
  87.6 165.7 %copy-start.7 = (f32[4,4]{1,0:T(4,128)S(1)}, f32[4,4]{1,0:T(4,128)}, u32[]{:S(2)}) copy-start(f32[4,4]{1,0:T(4,128)} %param.19) | copy-start | bytes 196
  255.2 74.7 %copy-start.4 = (f32[4,4,3,1024]{3,1,2,0:T(4,128)S(1)}, f32[4,4,3,1024]{3,1,2,0:T(4,128)}, u32[]{:S(2)}) copy-start(f32[4,4,3,1024]{3,1,2,0:T(4,128)} %get-tuple-element.154) | copy-start | bytes 589828
  255.2 75.5 %copy-start.6 = (f32[8,3,256]{2,0,1:T(8,128)S(1)}, f32[8,3,256]{2,0,1:T(8,128)}, u32[]{:S(2)}) copy-start(f32[8,3,256]{2,0,1:T(8,128)} %copy-done.5) | copy-start | bytes 73732
where the time goes:
time: 333 us; the launch traced here: 331 us
  other arithmetic  210 us (63%)
  local copies, waits for them, and re-layouts  64.3 us (19%)
  blocking collectives  37.7 us (11%)
  starting transfers between devices  11.3 us (3%)
  matrix products  3.48 us (1%)
    reduce_sum x12, other arithmetic, stokeslet(): out_x = jnp.sum(direct * forces[0][None, :] + tangent * delta_x, axis=1)  184 us
    pmax x1, blocking collectives, body(): top = lax.pmax(jnp.max(speed), ('cx', 'cy'))  37.7 us
    reduce_sum x8, other arithmetic, double_layer(): jnp.sum(scalar * delta_x, axis=1)  14.1 us
    ppermute x3, starting transfers between devices, with_halo(): after = lax.ppermute(initial, axis, down)  9.83 us
    slice x8, local copies, waits for them, and re-layouts, stokeslet(): forces[1][None, :]  7.5 us
  transfers between devices with their start and end apart: 6, of which 2 were waited for; matrix products, arithmetic and copies ran while one was open for 9% of the time, Pallas kernels for 0%

commit v1 on v0

v1 whole, which is shorter than its diff:
```python
import functools
import math

import jax
import jax.numpy as jnp
from jax import lax
from jax.experimental import pallas as pl
from jax.experimental.pallas import tpu as pltpu
from jax.sharding import PartitionSpec as P

HALO = 3
CHUNK = 256

soften = 0.25
stokes_scale = 1.0 / (8.0 * math.pi)
layer_scale = 3.0 / (4.0 * math.pi)

MESH = pl.DeviceIdType.MESH
f32 = jnp.float32
bf16 = jnp.bfloat16


def with_halo(value, sides, width):
    for axis, dim in sides:
        size, length = (lax.axis_size(axis), value.shape[dim])
        up = [(i, (i + 1) % size) for i in range(size)]
        down = [(j, i) for i, j in up]
        last = lax.slice_in_dim(value, length - width, length, axis=dim)
        initial = lax.slice_in_dim(value, 0, width, axis=dim)
        before = lax.ppermute(last, axis, up)
        after = lax.ppermute(initial, axis, down)
        value = jnp.concatenate([before, value, after], axis=dim)
    return value


def membrane(positions, analysis, stiffness, synthesis):
    points = positions.shape[-1]
    centred = positions - jnp.mean(positions, axis=-1, keepdims=True)
    flat = centred.reshape(-1, points).astype(jnp.bfloat16)
    coeff = jnp.dot(flat, analysis, preferred_element_type=jnp.float32)
    scaled = (coeff * stiffness[None, :]).astype(jnp.bfloat16)
    force = -jnp.dot(scaled, synthesis, preferred_element_type=jnp.float32)
    return force.reshape(positions.shape)


def local_slot(global_id, first_row, first_col, all_rows, all_cols, ext_cols):
    grid_row = global_id // all_cols
    grid_col = global_id % all_cols
    local_row = (grid_row - first_row + HALO) % all_rows
    local_col = (grid_col - first_col + HALO) % all_cols
    return local_row * ext_cols + local_col


def pieces(value):
    high = value.astype(bf16).astype(f32)
    rest = value - high
    middle = rest.astype(bf16).astype(f32)
    return high, middle, rest - middle


def rows8(points):
    return [jnp.broadcast_to(points[i : i + 1, :], (8, points.shape[1])) for i in range(3)]


def pick(row, values):
    out = jnp.zeros_like(values[0])
    for i, value in enumerate(values):
        out = jnp.where(row == i, value, out)
    return out


def target_features(points):
    x0, x1, x2 = rows8(points)
    row = lax.broadcasted_iota(jnp.int32, x0.shape, 0)
    square = x0 * x0 + x1 * x1 + x2 * x2
    high, middle, low = pieces(pick(row, [x0, x1, x2, square, jnp.ones_like(x0)]))
    return jnp.concatenate([high, high, middle, high, low, middle], axis=0).astype(bf16)


def source_side(value):
    high, middle, low = pieces(value)
    stacked = jnp.concatenate([high, middle, high, low, high, middle], axis=0)
    return stacked.T.astype(bf16)


def distance_features(y, row):
    y0, y1, y2 = y
    square = y0 * y0 + y1 * y1 + y2 * y2 + soften
    return source_side(pick(row, [-2.0 * y0, -2.0 * y1, -2.0 * y2, jnp.ones_like(y0), square]))


def stokes_prepare(source, force, side_ref, direct_ref, coef_ref, base):
    y = rows8(source)
    f = rows8(force)
    row = lax.broadcasted_iota(jnp.int32, y[0].shape, 0)
    side = distance_features(y, row)
    along = y[0] * f[0] + y[1] * f[1] + y[2] * f[2]
    f8 = pick(row % 4, [f[0], f[1], f[2], along])
    first = f8 * jnp.where(row < 4, 1.0, y[0])
    second = f8 * jnp.where(row < 4, y[1], y[2])
    direct = jnp.concatenate(pieces(f8)[:2], axis=0).astype(bf16)
    h1, m1, l1 = pieces(first)
    h2, m2, l2 = pieces(second)
    coef = jnp.concatenate([h1, h2, m1, m2, l1, l2], axis=0).astype(bf16)
    for c in range(side.shape[0] // CHUNK):
        part = slice(c * CHUNK, (c + 1) * CHUNK)
        side_ref[base + c] = side[part]
        direct_ref[base + c] = direct[:, part]
        coef_ref[base + c] = coef[:, part]


def stokes_chunks(features, side_ref, direct_ref, coef_ref, acc_ref, chunks, width):
    total = features.shape[1]
    acc_ref[...] = jnp.zeros_like(acc_ref)

    def step(c, carry):
        side = side_ref[c]
        direct = direct_ref[c]
        coef = coef_ref[c]
        for t in range(total // width):
            part = slice(t * width, (t + 1) * width)
            s = jnp.dot(side, features[:, part], preferred_element_type=f32)
            root = lax.rsqrt(s)
            cube = (root * root * root).astype(bf16)
            acc_ref[0:16, part] += jnp.dot(direct, root.astype(bf16), preferred_element_type=f32)
            acc_ref[16:64, part] += jnp.dot(coef, cube, preferred_element_type=f32)
        return carry

    lax.fori_loop(0, chunks, step, 0)


def stokes_finish(target, acc_ref):
    x = [target[i : i + 1, :] for i in range(3)]
    direct = acc_ref[0:8, :] + acc_ref[8:16, :]
    low = acc_ref[16:24, :] + (acc_ref[32:40, :] + acc_ref[48:56, :])
    high = acc_ref[24:32, :] + (acc_ref[40:48, :] + acc_ref[56:64, :])

    def contract(block, at):
        out = -block[at + 3 : at + 4]
        for j in range(3):
            out = out + x[j] * block[at + j : at + j + 1]
        return out

    line = contract(low, 0)
    turned = [contract(low, 4), contract(high, 0), contract(high, 4)]
    return [
        stokes_scale * (direct[i : i + 1] + soften * low[i : i + 1] + x[i] * line - turned[i])
        for i in range(3)
    ]


def cell_kernel(
    slot_ref, own_ref, drag_ref, target_ref, pos_ref, force_ref, out_ref, top_ref,
    side_ref, direct_ref, coef_ref, acc_ref, *, near
):
    cell = pl.program_id(0)
    target = target_ref[0]
    per_cell = pos_ref.shape[2] // CHUNK
    features = target_features(target)
    for n in range(near):
        slot = slot_ref[cell, n]
        stokes_prepare(pos_ref[slot], force_ref[slot], side_ref, direct_ref, coef_ref, n * per_cell)
    stokes_chunks(features, side_ref, direct_ref, coef_ref, acc_ref, near * per_cell, 256)
    own = force_ref[own_ref[cell]]
    drag = drag_ref[cell]
    parts = stokes_finish(target, acc_ref)
    square = jnp.zeros_like(parts[0])
    for i in range(3):
        value = drag * own[i : i + 1] + parts[i]
        out_ref[0, i : i + 1, :] = value
        square = square + value * value
    best = jnp.broadcast_to(jnp.max(square, axis=1, keepdims=True), (1, 128))

    @pl.when(cell == 0)
    def _():
        top_ref[...] = best

    @pl.when(cell > 0)
    def _():
        top_ref[...] = jnp.maximum(top_ref[...], best)


def cell_velocity(cells, drag, near_slots, own_slots, flat_pos, flat_force):
    count, _, points = cells.shape
    near = near_slots.shape[1]
    chunks = near * points // CHUNK
    whole = pl.BlockSpec(flat_pos.shape, lambda i, *_: (0, 0, 0), pipeline_mode=pl.Buffered(1))
    one = pl.BlockSpec((1, 3, points), lambda i, *_: (i, 0, 0))
    return pl.pallas_call(
        functools.partial(cell_kernel, near=near),
        grid_spec=pltpu.PrefetchScalarGridSpec(
            num_scalar_prefetch=3,
            grid=(count,),
            in_specs=[one, whole, whole],
            out_specs=[one, pl.BlockSpec((1, 128), lambda i, *_: (0, 0))],
            scratch_shapes=[
                pltpu.VMEM((chunks, CHUNK, 48), bf16),
                pltpu.VMEM((chunks, 16, CHUNK), bf16),
                pltpu.VMEM((chunks, 48, CHUNK), bf16),
                pltpu.VMEM((64, points), f32),
            ],
        ),
        out_shape=(
            jax.ShapeDtypeStruct(cells.shape, f32),
            jax.ShapeDtypeStruct((1, 128), f32),
        ),
        name="cell_velocity",
    )(near_slots, own_slots, drag, cells, flat_pos, flat_force)


def wall_kernel(
    cell_slot_ref, patch_slot_ref, target_ref, pos_ref, force_ref, wall_ref, out_ref,
    side_ref, direct_ref, coef_ref, acc_ref, *, near, listed
):
    patch = pl.program_id(0)
    target = target_ref[0]
    points = target.shape[1]
    per_cell = pos_ref.shape[2] // CHUNK
    features = target_features(target)
    for n in range(near):
        slot = cell_slot_ref[patch, n]
        stokes_prepare(pos_ref[slot], force_ref[slot], side_ref, direct_ref, coef_ref, n * per_cell)
    stokes_chunks(features, side_ref, direct_ref, coef_ref, acc_ref, near * per_cell, points)
    flow = stokes_finish(target, acc_ref)
    total = jnp.zeros((32, points), f32)
    for n in range(listed):
        source = wall_ref[patch_slot_ref[patch, n]]
        y = rows8(source[0:3])
        normal = rows8(source[3:6])
        value = rows8(source[6:9])
        weight = -layer_scale * jnp.broadcast_to(source[9:10], y[0].shape)
        value = [weight * v for v in value]
        row = lax.broadcasted_iota(jnp.int32, y[0].shape, 0)
        zero = jnp.zeros_like(y[0])

        def linear(v):
            return source_side(pick(row, [*v, zero, -(y[0] * v[0] + y[1] * v[1] + y[2] * v[2])]))

        s = jnp.dot(distance_features(y, row), features, preferred_element_type=f32)
        along_q = jnp.dot(linear(value), features, preferred_element_type=f32)
        along_n = jnp.dot(linear(normal), features, preferred_element_type=f32)
        root = lax.rsqrt(s)
        square = root * root
        scalar = (along_q * along_n * (square * square * root)).astype(bf16)
        high, middle, low = pieces(pick(row, [*y, jnp.ones_like(y[0])]))
        coef = jnp.concatenate([high, middle, low, zero], axis=0).astype(bf16)
        total = total + jnp.dot(coef, scalar, preferred_element_type=f32)
    moment = total[0:8] + (total[8:16] + total[16:24])
    for i in range(3):
        layer = target[i : i + 1] * moment[3:4] - moment[i : i + 1]
        out_ref[0, i : i + 1, :] = 2.0 * layer + 2.0 * flow[i]


def wall_density(wall_pos, cell_slots, patch_slots, flat_pos, flat_force, ext_wall):
    count, _, points = wall_pos.shape
    near, listed = cell_slots.shape[1], patch_slots.shape[1]
    chunks = near * flat_pos.shape[2] // CHUNK
    whole = pl.BlockSpec(flat_pos.shape, lambda i, *_: (0, 0, 0), pipeline_mode=pl.Buffered(1))
    walls = pl.BlockSpec(ext_wall.shape, lambda i, *_: (0, 0, 0), pipeline_mode=pl.Buffered(1))
    one = pl.BlockSpec((1, 3, points), lambda i, *_: (i, 0, 0))
    return pl.pallas_call(
        functools.partial(wall_kernel, near=near, listed=listed),
        grid_spec=pltpu.PrefetchScalarGridSpec(
            num_scalar_prefetch=2,
            grid=(count,),
            in_specs=[one, whole, whole, walls],
            out_specs=one,
            scratch_shapes=[
                pltpu.VMEM((chunks, CHUNK, 48), bf16),
                pltpu.VMEM((chunks, 16, CHUNK), bf16),
                pltpu.VMEM((chunks, 48, CHUNK), bf16),
                pltpu.VMEM((64, points), f32),
            ],
        ),
        out_shape=jax.ShapeDtypeStruct(wall_pos.shape, f32),
        name="wall_density",
    )(cell_slots, patch_slots, wall_pos, flat_pos, flat_force, ext_wall)


def top_kernel(size_x, size_y, mine_ref, out_ref, row_ref, from_y, from_x, send_y, recv_y, send_x, recv_x):
    me_x, me_y = lax.axis_index("cx"), lax.axis_index("cy")
    barrier = pltpu.get_barrier_semaphore()
    for d in range(1, size_y):
        pl.semaphore_signal(
            barrier, inc=1, device_id=(me_x, lax.rem(me_y + d, size_y)), device_id_type=MESH
        )
    for d in range(1, size_x):
        pl.semaphore_signal(
            barrier, inc=1, device_id=(lax.rem(me_x + d, size_x), me_y), device_id_type=MESH
        )
    pl.semaphore_wait(barrier, size_x + size_y - 2)
    copies = []
    for d in range(1, size_y):
        copy = pltpu.make_async_remote_copy(
            src_ref=mine_ref,
            dst_ref=from_y.at[d - 1],
            send_sem=send_y.at[d - 1],
            recv_sem=recv_y.at[d - 1],
            device_id=(me_x, lax.rem(me_y + d, size_y)),
            device_id_type=MESH,
        )
        copy.start()
        copies.append(copy)
    best = mine_ref[...]
    for d, copy in enumerate(copies):
        copy.wait()
        best = jnp.maximum(best, from_y[d])
    row_ref[...] = best
    copies = []
    for d in range(1, size_x):
        copy = pltpu.make_async_remote_copy(
            src_ref=row_ref,
            dst_ref=from_x.at[d - 1],
            send_sem=send_x.at[d - 1],
            recv_sem=recv_x.at[d - 1],
            device_id=(lax.rem(me_x + d, size_x), me_y),
            device_id_type=MESH,
        )
        copy.start()
        copies.append(copy)
    for d, copy in enumerate(copies):
        copy.wait()
        best = jnp.maximum(best, from_x[d])
    out_ref[...] = best


def top_of_all(mine, size_x, size_y):
    dma = pltpu.SemaphoreType.DMA
    return pl.pallas_call(
        functools.partial(top_kernel, size_x, size_y),
        out_shape=jax.ShapeDtypeStruct(mine.shape, f32),
        in_specs=[pl.BlockSpec(memory_space=pltpu.VMEM)],
        out_specs=pl.BlockSpec(memory_space=pltpu.VMEM),
        scratch_shapes=[
            pltpu.VMEM(mine.shape, f32),
            pltpu.VMEM((size_y - 1, *mine.shape), f32),
            pltpu.VMEM((size_x - 1, *mine.shape), f32),
            dma((size_y - 1,)),
            dma((size_y - 1,)),
            dma((size_x - 1,)),
            dma((size_x - 1,)),
        ],
        compiler_params=pltpu.CompilerParams(collective_id=0, has_side_effects=True),
        name="top_of_all",
    )(mine)


def body(
    cell_pos,
    cell_drag,
    cell_near,
    analysis,
    stiffness,
    synthesis,
    wall_pos,
    wall_normal,
    wall_weight,
    density,
    patch_near,
    cell_to_patch,
):
    row_count = cell_pos.shape[0]
    col_count = cell_pos.shape[1]
    points = cell_pos.shape[3]
    ext_cols = col_count + 2 * HALO
    all_rows = row_count * lax.axis_size("cx")
    all_cols = col_count * lax.axis_size("cy")
    first_row = lax.axis_index("cx") * row_count
    first_col = lax.axis_index("cy") * col_count
    slot = functools.partial(
        local_slot,
        first_row=first_row,
        first_col=first_col,
        all_rows=all_rows,
        all_cols=all_cols,
        ext_cols=ext_cols,
    )
    ext_pos = with_halo(cell_pos, (("cx", 0), ("cy", 1)), HALO)
    ext_force = membrane(ext_pos, analysis, stiffness, synthesis)
    flat_pos = ext_pos.reshape(-1, 3, points)
    flat_force = ext_force.reshape(-1, 3, points)
    count = row_count * col_count
    near_slots = slot(cell_near).reshape(count, -1)
    ids = jnp.arange(count, dtype=jnp.int32)
    own_slots = (ids // col_count + HALO) * ext_cols + ids % col_count + HALO
    velocity, top_square = cell_velocity(
        cell_pos.reshape(count, 3, points),
        cell_drag.reshape(count),
        near_slots,
        own_slots,
        flat_pos,
        flat_force,
    )
    top = jnp.sqrt(top_of_all(top_square, lax.axis_size("cx"), lax.axis_size("cy"))[0, 0])
    step = 1.0 / (top + 1e-06)
    moved_cells = cell_pos + step * velocity.reshape(cell_pos.shape)
    patch_count = wall_pos.shape[0]
    packed = jnp.concatenate([wall_pos, wall_normal, density, wall_weight[:, None, :]], axis=1)
    ext_wall = with_halo(packed, ((("cx", "cy"), 0),), patch_count)
    all_patches = patch_count * lax.axis_size(("cx", "cy"))
    block_start = lax.axis_index(("cx", "cy")) * patch_count
    own_patches = jnp.arange(patch_count, dtype=jnp.int32) + patch_count
    other_slots = (patch_near - block_start + patch_count) % all_patches
    chosen = jnp.concatenate([own_patches[:, None], other_slots], axis=1)
    density_next = wall_density(
        wall_pos, slot(cell_to_patch), chosen, flat_pos, flat_force, ext_wall
    )
    return (moved_cells, density_next)


def solution(mesh):
    placed = (
        P("cx", "cy", None, None),
        P("cx", "cy"),
        P("cx", "cy", None),
        P(),
        P(),
        P(),
        P(("cx", "cy"), None, None),
        P(("cx", "cy"), None, None),
        P(("cx", "cy"), None),
        P(("cx", "cy"), None, None),
        P(("cx", "cy"), None),
        P(("cx", "cy"), None),
    )
    return jax.shard_map(
        body,
        mesh=mesh,
        in_specs=placed,
        out_specs=(P("cx", "cy", None, None), P(("cx", "cy"), None, None)),
        check_vma=False,
    )
```

time: 333 us -> 228 us (0.68)
  other arithmetic: 210 us -> 9.83 us
  Pallas kernels: 0 us -> 170 us
  local copies, waits for them, and re-layouts: 64.3 us -> 21.3 us
  blocking collectives: 37.7 us -> 0 us
  waiting for transfers between devices: 2.01 us -> 6.96 us
    reduce_sum x21 -> x0, other arithmetic: 199 us -> none  [the longest x12 184 us: stokeslet(): out_x = jnp.sum(direct * forces[0][None, :] + tangent * delta_x, axis=1)]
    pallas_call x0 -> x3, Pallas kernels: none -> 170 us  [the longest x1 124 us: cell_velocity(): pl.pallas_call(functools.partial(cell_kernel, near=near), grid_spec=pltpu...]
    pmax x1 -> x0, blocking collectives: 37.7 us -> none  [body(): top = lax.pmax(jnp.max(speed), ('cx', 'cy'))]
    slice x25 -> x0, local copies, waits for them, and re-layouts: 20.4 us -> none  [the longest x8 7.5 us: stokeslet(): forces[1][None, :]]
    gather x9 -> x0, local copies, waits for them, and re-layouts: 16.5 us -> none  [the longest x2 4.11 us: body(): source_force = spread_many(flat_force[near_slots])]
    reshape x6 -> x2, local copies, waits for them, and re-layouts: 7.7 us -> 1.31 us  [the longest x1 0.69 us: body(): near_slots = slot(cell_near).reshape(count, -1)]
    ppermute x3, waiting for transfers between devices: 2.01 us -> 6.95 us  [with_halo(): before = lax.ppermute(last, axis, up)]
    unnamed x23 -> x19, local copies, waits for them, and re-layouts: 3.26 us -> 7.17 us
  transfers between devices with their start and end apart: 6 -> 6, of which waited for: 2 -> 2; matrix products, arithmetic and copies ran while one was open for 9% -> 5% of each run, Pallas kernels for 0% -> 0%
where the time goes in v1:
time: 228 us; the launch traced here: 227 us
  Pallas kernels  170 us (75%)
  local copies, waits for them, and re-layouts  21.3 us (9%)
  starting transfers between devices  13 us (6%)
  other arithmetic  9.83 us (4%)
  waiting for transfers between devices  6.96 us (3%)
  matrix products  4.15 us (2%)
    pallas_call x1, Pallas kernels, cell_velocity(): pl.pallas_call(functools.partial(cell_kernel, near=near), grid_spec=pltpu...  124 us
    pallas_call x1, Pallas kernels, wall_density(): pl.pallas_call(functools.partial(wall_kernel, near=near, listed=listed),...  35.6 us
    ppermute x3, starting transfers between devices, with_halo(): after = lax.ppermute(initial, axis, down)  12.4 us
    pallas_call x1, Pallas kernels, top_of_all(): pl.pallas_call(functools.partial(top_kernel, size_x, size_y), out_shape=j...  10.2 us
    unnamed x19, local copies, waits for them, and re-layouts  7.17 us
    ppermute x3, waiting for transfers between devices, with_halo(): before = lax.ppermute(last, axis, up)  6.95 us
  transfers between devices with their start and end apart: 6, of which 2 were waited for; matrix products, arithmetic and copies ran while one was open for 5% of the time, Pallas kernels for 0%

profile of v1, /device:TPU:0, one launch (start us, length us, event | category | flops | bytes accessed | tf_op | source)
XLA Modules:
  0.0 226.8 jit_solution(12504217336245519982)
XLA Ops:
  0.6 0.9 copy.60.target_ref
  4.4 6.0 %collective-permute-start.5 = (f32[8,10,256]{2,1,0:T(8,128)S(1)}, f32[8,10,256]{2,1,0:T(8,128)}, u32[]{:S(2)}, u32[]{:S(2)}) collective-permute-start(f32[8,10,256]{2,1,0:T(8,128)S(1)} %pad_maximum_fusion.2), channel_id=1, source_target_pairs={{1,0},{2,1},{3,2},{4,3},{5,4},{6,5},{7,6},{8,7},{9,8},{10,9},{11,1... | collective-permute-start | bytes 245768 | tf_op jit(solution)/shard_map/ppermute | solution.py:31
  10.4 1.0 fusion.25
  11.5 4.7 %collective-permute-start.1 = (f32[3,4,3,1024]{3,1,2,0:T(4,128)S(1)}, f32[3,4,3,1024]{3,1,2,0:T(4,128)S(1)}, u32[]{:S(2)}, u32[]{:S(2)}) collective-permute-start(f32[3,4,3,1024]{3,1,2,0:T(4,128)S(1)} %get-tuple-element.16), channel_id=1, source_target_pairs={{4,0},{8,4},{12,8},{16,12},{20,16},{24,20},{28,24},{0,28},{5,1},{9... | collective-permute-start | bytes 442376 | tf_op jit(solution)/shard_map/ppermute | solution.py:31
  19.3 1.0 constant_dynamic-update-slice_fusion.1
  20.3 1.2 fusion.24
  21.6 1.7 collective-permute-start.3
  23.3 0.8 copy.46
  26.7 1.8 pad_maximum_fusion.1.wall_ref
  28.5 6.7 %collective-permute-done.2 = f32[10,3,3,1024]{3,1,2,0:T(4,128)S(1)} collective-permute-done((f32[10,3,3,1024]{3,1,2,0:T(4,128)}, f32[10,3,3,1024]{3,1,2,0:T(4,128)S(1)}, u32[]{:S(2)}, u32[]{:S(2)}) %collective-permute-start.2) | collective-permute-done | bytes 368672 | tf_op jit(solution)/shard_map/ppermute | solution.py:30
  35.2 2.3 fusion.23
  37.4 2.1 copy.47
  39.5 2.3 %concatenate.19 = f32[300,1024]{1,0:T(8,128)S(1)} reshape(f32[10,10,3,1024]{3,2,1,0:T(4,128)} %copy.47) | data formatting | bytes 2457600 | tf_op jit(solution)/shard_map/concatenate | solution.py:32
  41.9 1.3 broadcast_multiply_fusion.1
  43.2 1.5 copy.49
  44.7 1.1 div.54
  45.8 4.1 %convolution_negate_fusion = f32[300,1024]{1,0:T(8,128)} fusion(bf16[1024,1024]{1,0:T(8,128)(2,1)S(1)} %copy-done, bf16[1024,1024]{1,0:T(8,128)(2,1)} %param.15, f32[300,1024]{1,0:T(8,128)S(1)} %concatenate.19, f32[1024]{0:T(1024)S(1)} %copy-done.4, f32[300]{0:T(512)S(1)} %div.54), kind=kOutput, calls=%fused_computation.2 | convolution fusion | flops 1259827200 | bytes 6657200 | tf_op jit(solution)/shard_map/dot_general | solution.py:42
  49.9 2.9 %reshape_reshape.3.force_ref = f32[100,3,1024]{2,1,0:T(4,128)} reshape(f32[300,1024]{1,0:T(8,128)} %convolution_negate_fusion) | data formatting | bytes 2457600 | tf_op jit(solution)/shard_map/reshape;reshape | solution.py:381
  52.9 124.1 %cell_velocity.1 = (f32[16,3,1024]{2,1,0:T(4,128)}, f32[1,128]{1,0:T(1,128)}) custom-call(s32[16,2]{1,0:T(8,128)} %bitcast.12, s32[16]{0:T(128)} %fusion.20.own_ref, f32[16]{0:T(128)} %reshape.44.drag_ref, f32[16,3,1024]{2,1,0:T(4,128)} %bitcast.11, f32[100,3,1024]{2,1,0:T(4,128)} %bitcast.8, f32[100,3,1024]{2,1,0:T(4,128)} %reshape_reshape.3.force_ref), custom_call_target="tpu_custom_call" | custom-call | tf_op jit(solution)/shard_map/cell_velocity/pallas_call | solution.py:189
  176.9 10.2 %top_of_all.1 = f32[1,128]{1,0:T(1,128)} custom-call(f32[1,128]{1,0:T(1,128)} %get-tuple-element.4.mine_ref), custom_call_target="tpu_custom_call" | custom-call | tf_op jit(solution)/shard_map/top_of_all/pallas_call | solution.py:329
  187.9 1.0 broadcast_multiply_fusion
  188.9 0.8 copy_add_fusion
  189.8 35.6 %wall_density.1 = f32[8,3,256]{2,1,0:T(4,128)} custom-call(s32[8,2]{1,0:T(8,128)} %fusion.9.cell_slot_ref, s32[8,5]{1,0:T(8,128)} %pad_add_fusion.patch_slot_ref, f32[8,3,256]{2,1,0:T(4,128)} %copy-done.2, f32[100,3,1024]{2,1,0:T(4,128)} %bitcast.9, f32[100,3,1024]{2,1,0:T(4,128)} %reshape_reshape.3.force_ref, f32[24,10,256]{2,1,0:T(8,128)} %pad_maximum_fusion.1.wall_ref), custom_call_target="tpu_custom_call" | custom-call | tf_op jit(solution)/shard_map/wall_density/pallas_call | solution.py:261
  225.4 1.4 copy.61
  (34 shorter events, 8.6 us)
Async XLA Ops:
  0.6 45.1 %copy-start = (bf16[1024,1024]{1,0:T(8,128)(2,1)S(1)}, bf16[1024,1024]{1,0:T(8,128)(2,1)}, u32[]{:S(2)}) copy-start(bf16[1024,1024]{1,0:T(8,128)(2,1)} %param.17) | copy-start | bytes 6291460
  1.5 25.1 %copy-start.2 = (f32[8,3,256]{2,1,0:T(4,128)}, f32[8,3,256]{2,1,0:T(4,128)S(1)}, u32[]{:S(2)}) copy-start(f32[8,3,256]{2,1,0:T(4,128)S(1)} %copy.60.target_ref) | copy-start | bytes 73732
  2.3 21.0 %copy-start.1 = (f32[4,4,3,1024]{3,1,2,0:T(4,128)S(1)}, f32[4,4,3,1024]{3,1,2,0:T(4,128)}, u32[]{:S(2)}) copy-start(f32[4,4,3,1024]{3,1,2,0:T(4,128)} %param.12) | copy-start | bytes 589828
  3.9 21.0 %copy-start.3 = (f32[4,4]{1,0:T(4,128)S(1)}, f32[4,4]{1,0:T(4,128)}, u32[]{:S(2)}) copy-start(f32[4,4]{1,0:T(4,128)} %param.13) | copy-start | bytes 196
  3.9 22.8 %collective-permute-start.4 = (f32[8,10,256]{2,1,0:T(8,128)S(1)}, f32[8,10,256]{2,1,0:T(8,128)}, u32[]{:S(2)}, u32[]{:S(2)}) collective-permute-start(f32[8,10,256]{2,1,0:T(8,128)S(1)} %pad_maximum_fusion.2), channel_id=1, source_target_pairs={{0,1},{1,2},{2,3},{3,4},{4,5},{5,6},{6,7},{7,8},{8,9},{9,10},{10,1... | collective-permute-start | bytes 245768 | tf_op jit(solution)/shard_map/ppermute | solution.py:30
  4.4 22.2 %collective-permute-start.5 = (f32[8,10,256]{2,1,0:T(8,128)S(1)}, f32[8,10,256]{2,1,0:T(8,128)}, u32[]{:S(2)}, u32[]{:S(2)}) collective-permute-start(f32[8,10,256]{2,1,0:T(8,128)S(1)} %pad_maximum_fusion.2), channel_id=1, source_target_pairs={{1,0},{2,1},{3,2},{4,3},{5,4},{6,5},{7,6},{8,7},{9,8},{10,9},{11,1... | collective-permute-start | bytes 245768 | tf_op jit(solution)/shard_map/ppermute | solution.py:31
  11.4 7.9 %collective-permute-start = (f32[3,4,3,1024]{3,1,2,0:T(4,128)S(1)}, f32[3,4,3,1024]{3,1,2,0:T(4,128)S(1)}, u32[]{:S(2)}, u32[]{:S(2)}) collective-permute-start(f32[3,4,3,1024]{3,1,2,0:T(4,128)S(1)} %get-tuple-element.17), channel_id=1, source_target_pairs={{0,4},{4,8},{8,12},{12,16},{16,20},{20,24},{24,28},{28,0},{1,5},{5... | collective-permute-start | bytes 442376 | tf_op jit(solution)/shard_map/ppermute | solution.py:30
  11.5 8.8 %collective-permute-start.1 = (f32[3,4,3,1024]{3,1,2,0:T(4,128)S(1)}, f32[3,4,3,1024]{3,1,2,0:T(4,128)S(1)}, u32[]{:S(2)}, u32[]{:S(2)}) collective-permute-start(f32[3,4,3,1024]{3,1,2,0:T(4,128)S(1)} %get-tuple-element.16), channel_id=1, source_target_pairs={{4,0},{8,4},{12,8},{16,12},{20,16},{24,20},{28,24},{0,28},{5,1},{9... | collective-permute-start | bytes 442376 | tf_op jit(solution)/shard_map/ppermute | solution.py:31
  21.6 13.6 %collective-permute-start.2 = (f32[10,3,3,1024]{3,1,2,0:T(4,128)}, f32[10,3,3,1024]{3,1,2,0:T(4,128)S(1)}, u32[]{:S(2)}, u32[]{:S(2)}) collective-permute-start(f32[10,3,3,1024]{3,1,2,0:T(4,128)} %get-tuple-element.14), channel_id=1, source_target_pairs={{0,1},{1,2},{2,3},{3,0},{4,5},{5,6},{6,7},{7,4},{8,9},{9,10},{10,1... | collective-permute-start | bytes 1105928 | tf_op jit(solution)/shard_map/ppermute | solution.py:30
  21.6 13.6 %collective-permute-start.3 = (f32[10,3,3,1024]{3,1,2,0:T(4,128)}, f32[10,3,3,1024]{3,1,2,0:T(4,128)}, u32[]{:S(2)}, u32[]{:S(2)}) collective-permute-start(f32[10,3,3,1024]{3,1,2,0:T(4,128)} %get-tuple-element.15), channel_id=1, source_target_pairs={{1,0},{2,1},{3,2},{0,3},{5,4},{6,5},{7,6},{4,7},{9,8},{10,9},{11,1... | collective-permute-start | bytes 1105928 | tf_op jit(solution)/shard_map/ppermute | solution.py:31
  39.5 6.3 %copy-start.4 = (f32[1024]{0:T(1024)S(1)}, f32[1024]{0:T(1024)}, u32[]{:S(2)}) copy-start(f32[1024]{0:T(1024)} %param.16) | copy-start | bytes 12292

commit v2 on v1

--- a/solution.py
+++ b/solution.py
@@ -9,7 +9,7 @@
 from jax.sharding import PartitionSpec as P
 
 HALO = 3
-CHUNK = 256
+WIDTH = 512
 
 soften = 0.25
 stokes_scale = 1.0 / (8.0 * math.pi)
@@ -89,51 +89,39 @@
     return source_side(pick(row, [-2.0 * y0, -2.0 * y1, -2.0 * y2, jnp.ones_like(y0), square]))
 
 
-def stokes_prepare(source, force, side_ref, direct_ref, coef_ref, base):
+def stokes_prepare(source, force, side_ref, coef_ref, base):
     y = rows8(source)
     f = rows8(force)
     row = lax.broadcasted_iota(jnp.int32, y[0].shape, 0)
-    side = distance_features(y, row)
     along = y[0] * f[0] + y[1] * f[1] + y[2] * f[2]
+    square = y[0] * y[0] + y[1] * y[1] + y[2] * y[2]
     f8 = pick(row % 4, [f[0], f[1], f[2], along])
-    first = f8 * jnp.where(row < 4, 1.0, y[0])
-    second = f8 * jnp.where(row < 4, y[1], y[2])
-    direct = jnp.concatenate(pieces(f8)[:2], axis=0).astype(bf16)
-    h1, m1, l1 = pieces(first)
-    h2, m2, l2 = pieces(second)
-    coef = jnp.concatenate([h1, h2, m1, m2, l1, l2], axis=0).astype(bf16)
-    for c in range(side.shape[0] // CHUNK):
-        part = slice(c * CHUNK, (c + 1) * CHUNK)
-        side_ref[base + c] = side[part]
-        direct_ref[base + c] = direct[:, part]
-        coef_ref[base + c] = coef[:, part]
-
-
-def stokes_chunks(features, side_ref, direct_ref, coef_ref, acc_ref, chunks, width):
-    total = features.shape[1]
-    acc_ref[...] = jnp.zeros_like(acc_ref)
-
-    def step(c, carry):
-        side = side_ref[c]
-        direct = direct_ref[c]
-        coef = coef_ref[c]
-        for t in range(total // width):
-            part = slice(t * width, (t + 1) * width)
-            s = jnp.dot(side, features[:, part], preferred_element_type=f32)
-            root = lax.rsqrt(s)
-            cube = (root * root * root).astype(bf16)
-            acc_ref[0:16, part] += jnp.dot(direct, root.astype(bf16), preferred_element_type=f32)
-            acc_ref[16:64, part] += jnp.dot(coef, cube, preferred_element_type=f32)
-        return carry
-
-    lax.fori_loop(0, chunks, step, 0)
+    h1, m1, l1 = pieces(f8 * jnp.where(row < 4, 1.0, y[0]))
+    h2, m2, l2 = pieces(f8 * jnp.where(row < 4, y[1], y[2]))
+    h3, m3, l3 = pieces(f8 * square)
+    points = source.shape[1]
+    side_ref[base : base + points] = distance_features(y, row)
+    coef_ref[:, base : base + points] = jnp.concatenate(
+        [h1, h2, h3, m1, m2, m3, l1, l2, l3], axis=0
+    ).astype(bf16)
+
+
+def stokes_sums(features, side_ref, coef_ref, acc_ref, width):
+    side = side_ref[...]
+    coef = coef_ref[...]
+    for t in range(features.shape[1] // width):
+        part = slice(t * width, (t + 1) * width)
+        root = lax.rsqrt(jnp.dot(side, features[:, part], preferred_element_type=f32))
+        cube = (root * root * root).astype(bf16)
+        acc_ref[:, part] = jnp.dot(coef, cube, preferred_element_type=f32)
 
 
 def stokes_finish(target, acc_ref):
     x = [target[i : i + 1, :] for i in range(3)]
-    direct = acc_ref[0:8, :] + acc_ref[8:16, :]
-    low = acc_ref[16:24, :] + (acc_ref[32:40, :] + acc_ref[48:56, :])
-    high = acc_ref[24:32, :] + (acc_ref[40:48, :] + acc_ref[56:64, :])
+    low = acc_ref[0:8, :] + (acc_ref[24:32, :] + acc_ref[48:56, :])
+    high = acc_ref[8:16, :] + (acc_ref[32:40, :] + acc_ref[56:64, :])
+    far = acc_ref[16:24, :] + (acc_ref[40:48, :] + acc_ref[64:72, :])
+    square = x[0] * x[0] + x[1] * x[1] + x[2] * x[2] + 2.0 * soften
 
     def contract(block, at):
         out = -block[at + 3 : at + 4]
@@ -143,24 +131,26 @@
 
     line = contract(low, 0)
     turned = [contract(low, 4), contract(high, 0), contract(high, 4)]
-    return [
-        stokes_scale * (direct[i : i + 1] + soften * low[i : i + 1] + x[i] * line - turned[i])
-        for i in range(3)
-    ]
+    out = []
+    for i in range(3):
+        cross = x[0] * low[4 + i : 5 + i] + x[1] * high[i : i + 1] + x[2] * high[4 + i : 5 + i]
+        direct = square * low[i : i + 1] + far[i : i + 1] - 2.0 * cross
+        out.append(stokes_scale * (direct + x[i] * line - turned[i]))
+    return out
 
 
 def cell_kernel(
     slot_ref, own_ref, drag_ref, target_ref, pos_ref, force_ref, out_ref, top_ref,
-    side_ref, direct_ref, coef_ref, acc_ref, *, near
+    side_ref, coef_ref, acc_ref, *, near
 ):
     cell = pl.program_id(0)
     target = target_ref[0]
-    per_cell = pos_ref.shape[2] // CHUNK
+    per_cell = pos_ref.shape[2]
     features = target_features(target)
     for n in range(near):
         slot = slot_ref[cell, n]
-        stokes_prepare(pos_ref[slot], force_ref[slot], side_ref, direct_ref, coef_ref, n * per_cell)
-    stokes_chunks(features, side_ref, direct_ref, coef_ref, acc_ref, near * per_cell, 256)
+        stokes_prepare(pos_ref[slot], force_ref[slot], side_ref, coef_ref, n * per_cell)
+    stokes_sums(features, side_ref, coef_ref, acc_ref, min(WIDTH, target.shape[1]))
     own = force_ref[own_ref[cell]]
     drag = drag_ref[cell]
     parts = stokes_finish(target, acc_ref)
@@ -183,7 +173,7 @@
 def cell_velocity(cells, drag, near_slots, own_slots, flat_pos, flat_force):
     count, _, points = cells.shape
     near = near_slots.shape[1]
-    chunks = near * points // CHUNK
+    sources = near * points
     whole = pl.BlockSpec(flat_pos.shape, lambda i, *_: (0, 0, 0), pipeline_mode=pl.Buffered(1))
     one = pl.BlockSpec((1, 3, points), lambda i, *_: (i, 0, 0))
     return pl.pallas_call(
@@ -194,10 +184,9 @@
             in_specs=[one, whole, whole],
             out_specs=[one, pl.BlockSpec((1, 128), lambda i, *_: (0, 0))],
             scratch_shapes=[
-                pltpu.VMEM((chunks, CHUNK, 48), bf16),
-                pltpu.VMEM((chunks, 16, CHUNK), bf16),
-                pltpu.VMEM((chunks, 48, CHUNK), bf16),
-                pltpu.VMEM((64, points), f32),
+                pltpu.VMEM((sources, 48), bf16),
+                pltpu.VMEM((72, sources), bf16),
+                pltpu.VMEM((72, points), f32),
             ],
         ),
         out_shape=(
@@ -210,19 +199,18 @@
 
 def wall_kernel(
     cell_slot_ref, patch_slot_ref, target_ref, pos_ref, force_ref, wall_ref, out_ref,
-    side_ref, direct_ref, coef_ref, acc_ref, *, near, listed
+    side_ref, coef_ref, acc_ref, layer_ref, moment_ref, *, near, listed
 ):
     patch = pl.program_id(0)
     target = target_ref[0]
     points = target.shape[1]
-    per_cell = pos_ref.shape[2] // CHUNK
+    per_cell = pos_ref.shape[2]
     features = target_features(target)
     for n in range(near):
         slot = cell_slot_ref[patch, n]
-        stokes_prepare(pos_ref[slot], force_ref[slot], side_ref, direct_ref, coef_ref, n * per_cell)
-    stokes_chunks(features, side_ref, direct_ref, coef_ref, acc_ref, near * per_cell, points)
+        stokes_prepare(pos_ref[slot], force_ref[slot], side_ref, coef_ref, n * per_cell)
+    stokes_sums(features, side_ref, coef_ref, acc_ref, min(WIDTH, points))
     flow = stokes_finish(target, acc_ref)
-    total = jnp.zeros((32, points), f32)
     for n in range(listed):
         source = wall_ref[patch_slot_ref[patch, n]]
         y = rows8(source[0:3])
@@ -236,15 +224,18 @@
         def linear(v):
             return source_side(pick(row, [*v, zero, -(y[0] * v[0] + y[1] * v[1] + y[2] * v[2])]))
 
-        s = jnp.dot(distance_features(y, row), features, preferred_element_type=f32)
-        along_q = jnp.dot(linear(value), features, preferred_element_type=f32)
-        along_n = jnp.dot(linear(normal), features, preferred_element_type=f32)
-        root = lax.rsqrt(s)
-        square = root * root
-        scalar = (along_q * along_n * (square * square * root)).astype(bf16)
+        part = slice(n * points, (n + 1) * points)
+        layer_ref[0, part] = distance_features(y, row)
+        layer_ref[1, part] = linear(value)
+        layer_ref[2, part] = linear(normal)
         high, middle, low = pieces(pick(row, [*y, jnp.ones_like(y[0])]))
-        coef = jnp.concatenate([high, middle, low, zero], axis=0).astype(bf16)
-        total = total + jnp.dot(coef, scalar, preferred_element_type=f32)
+        moment_ref[:, part] = jnp.concatenate([high, middle, low, zero], axis=0).astype(bf16)
+    root = lax.rsqrt(jnp.dot(layer_ref[0], features, preferred_element_type=f32))
+    along_q = jnp.dot(layer_ref[1], features, preferred_element_type=f32)
+    along_n = jnp.dot(layer_ref[2], features, preferred_element_type=f32)
+    square = root * root
+    scalar = (along_q * along_n * (square * square * root)).astype(bf16)
+    total = jnp.dot(moment_ref[...], scalar, preferred_element_type=f32)
     moment = total[0:8] + (total[8:16] + total[16:24])
     for i in range(3):
         layer = target[i : i + 1] * moment[3:4] - moment[i : i + 1]
@@ -254,7 +245,7 @@
 def wall_density(wall_pos, cell_slots, patch_slots, flat_pos, flat_force, ext_wall):
     count, _, points = wall_pos.shape
     near, listed = cell_slots.shape[1], patch_slots.shape[1]
-    chunks = near * flat_pos.shape[2] // CHUNK
+    sources = near * flat_pos.shape[2]
     whole = pl.BlockSpec(flat_pos.shape, lambda i, *_: (0, 0, 0), pipeline_mode=pl.Buffered(1))
     walls = pl.BlockSpec(ext_wall.shape, lambda i, *_: (0, 0, 0), pipeline_mode=pl.Buffered(1))
     one = pl.BlockSpec((1, 3, points), lambda i, *_: (i, 0, 0))
@@ -266,10 +257,11 @@
             in_specs=[one, whole, whole, walls],
             out_specs=one,
             scratch_shapes=[
-                pltpu.VMEM((chunks, CHUNK, 48), bf16),
-                pltpu.VMEM((chunks, 16, CHUNK), bf16),
-                pltpu.VMEM((chunks, 48, CHUNK), bf16),
-                pltpu.VMEM((64, points), f32),
+                pltpu.VMEM((sources, 48), bf16),
+                pltpu.VMEM((72, sources), bf16),
+                pltpu.VMEM((72, points), f32),
+                pltpu.VMEM((3, listed * points, 48), bf16),
+                pltpu.VMEM((32, listed * points), bf16),
             ],
         ),
         out_shape=jax.ShapeDtypeStruct(wall_pos.shape, f32),

time: 228 us -> 126 us (0.55)
  Pallas kernels: 170 us -> 68.2 us
    pallas_call x1, Pallas kernels: 124 us -> 40.4 us  [cell_velocity(): pl.pallas_call(functools.partial(cell_kernel, near=near), grid_spec=pltpu...]
    pallas_call x1, Pallas kernels: 35.6 us -> 17.6 us  [wall_density(): pl.pallas_call(functools.partial(wall_kernel, near=near, listed=listed),...]
  transfers between devices with their start and end apart: 6 -> 6, of which waited for: 2 -> 2; matrix products, arithmetic and copies ran while one was open for 5% -> 9% of each run, Pallas kernels for 0% -> 0%
where the time goes in v2:
time: 126 us; the launch traced here: 125 us
  Pallas kernels  68.2 us (54%)
  local copies, waits for them, and re-layouts  21.3 us (17%)
  starting transfers between devices  13 us (10%)
  other arithmetic  9.83 us (8%)
  waiting for transfers between devices  6.96 us (6%)
  matrix products  4.15 us (3%)
  between operations  1.52 us (1%)
    pallas_call x1, Pallas kernels, cell_velocity(): pl.pallas_call(functools.partial(cell_kernel, near=near), grid_spec=pltpu...  40.4 us
    pallas_call x1, Pallas kernels, wall_density(): pl.pallas_call(functools.partial(wall_kernel, near=near, listed=listed),...  17.6 us
    ppermute x3, starting transfers between devices, with_halo(): after = lax.ppermute(initial, axis, down)  12.4 us
    pallas_call x1, Pallas kernels, top_of_all(): pl.pallas_call(functools.partial(top_kernel, size_x, size_y), out_shape=j...  10.2 us
    unnamed x19, local copies, waits for them, and re-layouts  7.17 us
    ppermute x3, waiting for transfers between devices, with_halo(): before = lax.ppermute(last, axis, up)  6.95 us
    concatenate x3, local copies, waits for them, and re-layouts, with_halo(): value = jnp.concatenate([before, value, after], axis=dim)  4.43 us
    dot_general x1, matrix products, membrane(): force = -jnp.dot(scaled, synthesis, preferred_element_type=jnp.float32)  4.15 us
  transfers between devices with their start and end apart: 6, of which 2 were waited for; matrix products, arithmetic and copies ran while one was open for 9% of the time, Pallas kernels for 0%

profile of v2, /device:TPU:0, one launch (start us, length us, event | category | flops | bytes accessed | tf_op | source)
XLA Modules:
  0.0 125.1 jit_solution(17530203989209465720)
XLA Ops:
  0.6 0.9 copy.60.target_ref
  4.4 6.0 %collective-permute-start.5 = (f32[8,10,256]{2,1,0:T(8,128)S(1)}, f32[8,10,256]{2,1,0:T(8,128)}, u32[]{:S(2)}, u32[]{:S(2)}) collective-permute-start(f32[8,10,256]{2,1,0:T(8,128)S(1)} %pad_maximum_fusion.2), channel_id=1, source_target_pairs={{1,0},{2,1},{3,2},{4,3},{5,4},{6,5},{7,6},{8,7},{9,8},{10,9},{11,1... | collective-permute-start | bytes 245768 | tf_op jit(solution)/shard_map/ppermute | solution.py:31
  10.4 1.0 fusion.25
  11.5 4.7 %collective-permute-start.1 = (f32[3,4,3,1024]{3,1,2,0:T(4,128)S(1)}, f32[3,4,3,1024]{3,1,2,0:T(4,128)S(1)}, u32[]{:S(2)}, u32[]{:S(2)}) collective-permute-start(f32[3,4,3,1024]{3,1,2,0:T(4,128)S(1)} %get-tuple-element.16), channel_id=1, source_target_pairs={{4,0},{8,4},{12,8},{16,12},{20,16},{24,20},{28,24},{0,28},{5,1},{9... | collective-permute-start | bytes 442376 | tf_op jit(solution)/shard_map/ppermute | solution.py:31
  19.3 1.0 constant_dynamic-update-slice_fusion.1
  20.3 1.2 fusion.24
  21.6 1.7 %collective-permute-start.3 = (f32[10,3,3,1024]{3,1,2,0:T(4,128)}, f32[10,3,3,1024]{3,1,2,0:T(4,128)}, u32[]{:S(2)}, u32[]{:S(2)}) collective-permute-start(f32[10,3,3,1024]{3,1,2,0:T(4,128)} %get-tuple-element.15), channel_id=1, source_target_pairs={{1,0},{2,1},{3,2},{0,3},{5,4},{6,5},{7,6},{4,7},{9,8},{10,9},{11,1... | collective-permute-start | bytes 1105928 | tf_op jit(solution)/shard_map/ppermute | solution.py:31
  23.3 0.8 copy.46
  26.7 1.8 %pad_maximum_fusion.1.wall_ref = f32[24,10,256]{2,1,0:T(8,128)} fusion(f32[8,10,256]{2,1,0:T(8,128)} %collective-permute-done.5, f32[8,1,256]{2,1,0:T(1,128)S(1)} %broadcast_in_dim.2, f32[8,3,256]{2,1,0:T(4,128)S(1)} %copy.59, f32[8,3,256]{2,1,0:T(4,128)S(1)} %copy.58, f32[8,3,256]{2,1,0:T(4,128)S(1)} %copy.60.target_ref, f32[8,10,256]{2,1,0:T(8,128)} %collective-permute-done.4), kind=kLoop, calls=%fused_computation.7 | loop fusion | flops 307200 | bytes 491520 | tf_op jit(solution)/shard_map/concatenate | solution.py:32
  28.5 6.7 %collective-permute-done.2 = f32[10,3,3,1024]{3,1,2,0:T(4,128)S(1)} collective-permute-done((f32[10,3,3,1024]{3,1,2,0:T(4,128)}, f32[10,3,3,1024]{3,1,2,0:T(4,128)S(1)}, u32[]{:S(2)}, u32[]{:S(2)}) %collective-permute-start.2) | collective-permute-done | bytes 368672 | tf_op jit(solution)/shard_map/ppermute | solution.py:30
  35.2 2.3 %fusion.23 = (f32[10,10,3]{1,2,0:T(4,128)}, f32[10,10,3,1024]{3,1,2,0:T(8,128)S(1)}) fusion(f32[10,3,3,1024]{3,1,2,0:T(4,128)} %collective-permute-done.3, f32[10,4,3,1024]{3,1,2,0:T(4,128)S(1)} %constant_dynamic-update-slice_fusion, f32[10,3,3,1024]{3,1,2,0:T(4,128)S(1)} %collective-permute-done.2), kind=kLoop, calls=%fused_computation.67 | loop fusion | flops 921300 | bytes 2458800 | tf_op jit(solution)/shard_map/reduce_sum | solution.py:38
  37.4 2.1 %copy.47 = f32[10,10,3,1024]{3,2,1,0:T(4,128)} copy(f32[10,10,3,1024]{3,1,2,0:T(8,128)S(1)} %get-tuple-element.13) | data formatting | bytes 2457600 | tf_op jit(solution)/shard_map/concatenate | solution.py:32
  39.5 2.3 %concatenate.19 = f32[300,1024]{1,0:T(8,128)S(1)} reshape(f32[10,10,3,1024]{3,2,1,0:T(4,128)} %copy.47) | data formatting | bytes 2457600 | tf_op jit(solution)/shard_map/concatenate | solution.py:32
  41.9 1.3 %broadcast_multiply_fusion.1 = f32[10,10,3]{1,2,0:T(4,128)} fusion(f32[10,10,3]{1,2,0:T(4,128)} %get-tuple-element.12), kind=kLoop, calls=%fused_computation.11 | loop fusion | flops 300 | bytes 2400 | tf_op jit(solution)/shard_map/div | solution.py:38
  43.2 1.5 %copy.49 = f32[10,10,3]{2,1,0:T(8,128)} copy(f32[10,10,3]{1,2,0:T(4,128)} %broadcast_multiply_fusion.1) | data formatting | bytes 2400 | tf_op jit(solution)/shard_map/div | solution.py:38
  44.7 1.1 div.54
  45.8 4.1 %convolution_negate_fusion = f32[300,1024]{1,0:T(8,128)} fusion(bf16[1024,1024]{1,0:T(8,128)(2,1)S(1)} %copy-done, bf16[1024,1024]{1,0:T(8,128)(2,1)} %param.15, f32[300,1024]{1,0:T(8,128)S(1)} %concatenate.19, f32[1024]{0:T(1024)S(1)} %copy-done.4, f32[300]{0:T(512)S(1)} %div.54), kind=kOutput, calls=%fused_computation.2 | convolution fusion | flops 1259827200 | bytes 6657200 | tf_op jit(solution)/shard_map/dot_general | solution.py:42
  49.9 2.9 %reshape_reshape.3.force_ref = f32[100,3,1024]{2,1,0:T(4,128)} reshape(f32[300,1024]{1,0:T(8,128)} %convolution_negate_fusion) | data formatting | bytes 2457600 | tf_op jit(solution)/shard_map/reshape;reshape | solution.py:373
  52.9 40.4 %cell_velocity.1 = (f32[16,3,1024]{2,1,0:T(4,128)}, f32[1,128]{1,0:T(1,128)}) custom-call(s32[16,2]{1,0:T(8,128)} %bitcast.12, s32[16]{0:T(128)} %fusion.20.own_ref, f32[16]{0:T(128)} %reshape.44.drag_ref, f32[16,3,1024]{2,1,0:T(4,128)} %bitcast.11, f32[100,3,1024]{2,1,0:T(4,128)} %bitcast.8, f32[100,3,1024]{2,1,0:T(4,128)} %reshape_reshape.3.force_ref), custom_call_target="tpu_custom_call" | custom-call | tf_op jit(solution)/shard_map/cell_velocity/pallas_call | solution.py:179
  93.3 10.2 %top_of_all.1 = f32[1,128]{1,0:T(1,128)} custom-call(f32[1,128]{1,0:T(1,128)} %get-tuple-element.4.mine_ref), custom_call_target="tpu_custom_call" | custom-call | tf_op jit(solution)/shard_map/top_of_all/pallas_call | solution.py:321
  104.3 1.0 broadcast_multiply_fusion
  105.3 0.8 copy_add_fusion
  106.1 17.6 %wall_density.1 = f32[8,3,256]{2,1,0:T(4,128)} custom-call(s32[8,2]{1,0:T(8,128)} %fusion.9.cell_slot_ref, s32[8,5]{1,0:T(8,128)} %pad_add_fusion.patch_slot_ref, f32[8,3,256]{2,1,0:T(4,128)} %copy-done.2, f32[100,3,1024]{2,1,0:T(4,128)} %bitcast.9, f32[100,3,1024]{2,1,0:T(4,128)} %reshape_reshape.3.force_ref, f32[24,10,256]{2,1,0:T(8,128)} %pad_maximum_fusion.1.wall_ref), custom_call_target="tpu_custom_call" | custom-call | tf_op jit(solution)/shard_map/wall_density/pallas_call | solution.py:252
  123.7 1.4 %copy.61 = f32[8,3,256]{2,0,1:T(8,128)} copy(f32[8,3,256]{2,1,0:T(4,128)} %wall_density.1) | data formatting | bytes 49152
  (34 shorter events, 8.6 us)
Async XLA Ops:
  0.6 45.1 %copy-start = (bf16[1024,1024]{1,0:T(8,128)(2,1)S(1)}, bf16[1024,1024]{1,0:T(8,128)(2,1)}, u32[]{:S(2)}) copy-start(bf16[1024,1024]{1,0:T(8,128)(2,1)} %param.17) | copy-start | bytes 6291460
  1.5 25.1 %copy-start.2 = (f32[8,3,256]{2,1,0:T(4,128)}, f32[8,3,256]{2,1,0:T(4,128)S(1)}, u32[]{:S(2)}) copy-start(f32[8,3,256]{2,1,0:T(4,128)S(1)} %copy.60.target_ref) | copy-start | bytes 73732
  2.3 21.0 %copy-start.1 = (f32[4,4,3,1024]{3,1,2,0:T(4,128)S(1)}, f32[4,4,3,1024]{3,1,2,0:T(4,128)}, u32[]{:S(2)}) copy-start(f32[4,4,3,1024]{3,1,2,0:T(4,128)} %param.12) | copy-start | bytes 589828
  3.9 21.0 %copy-start.3 = (f32[4,4]{1,0:T(4,128)S(1)}, f32[4,4]{1,0:T(4,128)}, u32[]{:S(2)}) copy-start(f32[4,4]{1,0:T(4,128)} %param.13) | copy-start | bytes 196
  3.9 22.8 %collective-permute-start.4 = (f32[8,10,256]{2,1,0:T(8,128)S(1)}, f32[8,10,256]{2,1,0:T(8,128)}, u32[]{:S(2)}, u32[]{:S(2)}) collective-permute-start(f32[8,10,256]{2,1,0:T(8,128)S(1)} %pad_maximum_fusion.2), channel_id=1, source_target_pairs={{0,1},{1,2},{2,3},{3,4},{4,5},{5,6},{6,7},{7,8},{8,9},{9,10},{10,1... | collective-permute-start | bytes 245768 | tf_op jit(solution)/shard_map/ppermute | solution.py:30
  4.4 22.2 %collective-permute-start.5 = (f32[8,10,256]{2,1,0:T(8,128)S(1)}, f32[8,10,256]{2,1,0:T(8,128)}, u32[]{:S(2)}, u32[]{:S(2)}) collective-permute-start(f32[8,10,256]{2,1,0:T(8,128)S(1)} %pad_maximum_fusion.2), channel_id=1, source_target_pairs={{1,0},{2,1},{3,2},{4,3},{5,4},{6,5},{7,6},{8,7},{9,8},{10,9},{11,1... | collective-permute-start | bytes 245768 | tf_op jit(solution)/shard_map/ppermute | solution.py:31
  11.4 7.9 %collective-permute-start = (f32[3,4,3,1024]{3,1,2,0:T(4,128)S(1)}, f32[3,4,3,1024]{3,1,2,0:T(4,128)S(1)}, u32[]{:S(2)}, u32[]{:S(2)}) collective-permute-start(f32[3,4,3,1024]{3,1,2,0:T(4,128)S(1)} %get-tuple-element.17), channel_id=1, source_target_pairs={{0,4},{4,8},{8,12},{12,16},{16,20},{20,24},{24,28},{28,0},{1,5},{5... | collective-permute-start | bytes 442376 | tf_op jit(solution)/shard_map/ppermute | solution.py:30
  11.5 8.8 %collective-permute-start.1 = (f32[3,4,3,1024]{3,1,2,0:T(4,128)S(1)}, f32[3,4,3,1024]{3,1,2,0:T(4,128)S(1)}, u32[]{:S(2)}, u32[]{:S(2)}) collective-permute-start(f32[3,4,3,1024]{3,1,2,0:T(4,128)S(1)} %get-tuple-element.16), channel_id=1, source_target_pairs={{4,0},{8,4},{12,8},{16,12},{20,16},{24,20},{28,24},{0,28},{5,1},{9... | collective-permute-start | bytes 442376 | tf_op jit(solution)/shard_map/ppermute | solution.py:31
  21.6 13.6 %collective-permute-start.2 = (f32[10,3,3,1024]{3,1,2,0:T(4,128)}, f32[10,3,3,1024]{3,1,2,0:T(4,128)S(1)}, u32[]{:S(2)}, u32[]{:S(2)}) collective-permute-start(f32[10,3,3,1024]{3,1,2,0:T(4,128)} %get-tuple-element.14), channel_id=1, source_target_pairs={{0,1},{1,2},{2,3},{3,0},{4,5},{5,6},{6,7},{7,4},{8,9},{9,10},{10,1... | collective-permute-start | bytes 1105928 | tf_op jit(solution)/shard_map/ppermute | solution.py:30
  21.6 13.6 %collective-permute-start.3 = (f32[10,3,3,1024]{3,1,2,0:T(4,128)}, f32[10,3,3,1024]{3,1,2,0:T(4,128)}, u32[]{:S(2)}, u32[]{:S(2)}) collective-permute-start(f32[10,3,3,1024]{3,1,2,0:T(4,128)} %get-tuple-element.15), channel_id=1, source_target_pairs={{1,0},{2,1},{3,2},{0,3},{5,4},{6,5},{7,6},{4,7},{9,8},{10,9},{11,1... | collective-permute-start | bytes 1105928 | tf_op jit(solution)/shard_map/ppermute | solution.py:31
  39.5 6.3 %copy-start.4 = (f32[1024]{0:T(1024)S(1)}, f32[1024]{0:T(1024)}, u32[]{:S(2)}) copy-start(f32[1024]{0:T(1024)} %param.16) | copy-start | bytes 12292

commit v3 on v2

--- a/solution.py
+++ b/solution.py
@@ -20,27 +20,97 @@
 bf16 = jnp.bfloat16
 
 
-def with_halo(value, sides, width):
-    for axis, dim in sides:
-        size, length = (lax.axis_size(axis), value.shape[dim])
-        up = [(i, (i + 1) % size) for i in range(size)]
-        down = [(j, i) for i, j in up]
-        last = lax.slice_in_dim(value, length - width, length, axis=dim)
-        initial = lax.slice_in_dim(value, 0, width, axis=dim)
-        before = lax.ppermute(last, axis, up)
-        after = lax.ppermute(initial, axis, down)
-        value = jnp.concatenate([before, value, after], axis=dim)
-    return value
+def halo_kernel(size_x, size_y, cell_ref, wall_ref, ext_ref, walls_ref, send, recv, local):
+    me_x, me_y = lax.axis_index("cx"), lax.axis_index("cy")
+    rows, cols = cell_ref.shape[0], cell_ref.shape[1]
+    patches = wall_ref.shape[0]
+
+    def side(step, length):
+        if step == 1:
+            return slice(length - HALO, length), slice(0, HALO)
+        if step == 0:
+            return slice(0, length), slice(HALO, HALO + length)
+        return slice(0, HALO), slice(HALO + length, 2 * HALO + length)
+
+    pieces_out = []
+    for dx in (0, 1, -1):
+        for dy in (1, -1, 0):
+            if dx == 0 and dy == 0:
+                continue
+            device = (lax.rem(me_x + dx + size_x, size_x), lax.rem(me_y + dy + size_y, size_y))
+            (take_x, put_x), (take_y, put_y) = side(dx, rows), side(dy, cols)
+            pieces_out.append((cell_ref.at[take_x, take_y], ext_ref.at[put_x, put_y], device))
+    flat = me_x * size_y + me_y
+    for step, first in ((1, 0), (-1, 2 * patches)):
+        other = lax.rem(flat + step + size_x * size_y, size_x * size_y)
+        device = (other // size_y, lax.rem(other, size_y))
+        pieces_out.append((wall_ref, walls_ref.at[first : first + patches], device))
+
+    barrier = pltpu.get_barrier_semaphore()
+    for _, _, device in pieces_out:
+        pl.semaphore_signal(barrier, inc=1, device_id=device, device_id_type=MESH)
+    pl.semaphore_wait(barrier, len(pieces_out))
+    copies = []
+    for k, (src, dst, device) in enumerate(pieces_out):
+        copy = pltpu.make_async_remote_copy(
+            src_ref=src,
+            dst_ref=dst,
+            send_sem=send.at[k],
+            recv_sem=recv.at[k],
+            device_id=device,
+            device_id_type=MESH,
+        )
+        copy.start()
+        copies.append(copy)
+    own = ext_ref.at[HALO : HALO + rows, HALO : HALO + cols]
+    copies.append(pltpu.make_async_copy(cell_ref, own, local.at[0]))
+    copies[-1].start()
+    copies.append(pltpu.make_async_copy(wall_ref, walls_ref.at[patches : 2 * patches], local.at[1]))
+    copies[-1].start()
+    for copy in copies:
+        copy.wait()
+
+
+def halos(cells, walls, size_x, size_y):
+    rows, cols, _, points = cells.shape
+    dma = pltpu.SemaphoreType.DMA
+    return pl.pallas_call(
+        functools.partial(halo_kernel, size_x, size_y),
+        out_shape=(
+            jax.ShapeDtypeStruct((rows + 2 * HALO, cols + 2 * HALO, 3, points), f32),
+            jax.ShapeDtypeStruct((3 * walls.shape[0], *walls.shape[1:]), f32),
+        ),
+        in_specs=[pl.BlockSpec(memory_space=pltpu.VMEM)] * 2,
+        out_specs=[pl.BlockSpec(memory_space=pl.ANY)] * 2,
+        scratch_shapes=[dma((10,)), dma((10,)), dma((2,))],
+        compiler_params=pltpu.CompilerParams(collective_id=1, has_side_effects=True),
+        name="halos",
+    )(cells, walls)
+
+
+def membrane_kernel(pos_ref, analysis_ref, stiffness_ref, synthesis_ref, out_ref, flat_ref):
+    count = pos_ref.shape[0]
+    for c in range(count):
+        flat_ref[3 * c : 3 * c + 3, :] = pos_ref[c]
+    value = flat_ref[0 : 3 * count, :]
+    centred = (value - jnp.mean(value, axis=1, keepdims=True)).astype(bf16)
+    coeff = jnp.dot(centred, analysis_ref[...], preferred_element_type=f32)
+    scaled = (coeff * stiffness_ref[...]).astype(bf16)
+    flat_ref[0 : 3 * count, :] = -jnp.dot(scaled, synthesis_ref[...], preferred_element_type=f32)
+    for c in range(count):
+        out_ref[c] = flat_ref[3 * c : 3 * c + 3, :]
 
 
 def membrane(positions, analysis, stiffness, synthesis):
-    points = positions.shape[-1]
-    centred = positions - jnp.mean(positions, axis=-1, keepdims=True)
-    flat = centred.reshape(-1, points).astype(jnp.bfloat16)
-    coeff = jnp.dot(flat, analysis, preferred_element_type=jnp.float32)
-    scaled = (coeff * stiffness[None, :]).astype(jnp.bfloat16)
-    force = -jnp.dot(scaled, synthesis, preferred_element_type=jnp.float32)
-    return force.reshape(positions.shape)
+    count, _, points = positions.shape
+    return pl.pallas_call(
+        membrane_kernel,
+        out_shape=jax.ShapeDtypeStruct(positions.shape, f32),
+        in_specs=[pl.BlockSpec(memory_space=pltpu.VMEM)] * 4,
+        out_specs=pl.BlockSpec(memory_space=pltpu.VMEM),
+        scratch_shapes=[pltpu.VMEM((-(-3 * count // 8) * 8, points), f32)],
+        name="membrane",
+    )(positions, analysis, stiffness[None, :], synthesis)
 
 
 def local_slot(global_id, first_row, first_col, all_rows, all_cols, ext_cols):
@@ -367,10 +437,10 @@
         all_cols=all_cols,
         ext_cols=ext_cols,
     )
-    ext_pos = with_halo(cell_pos, (("cx", 0), ("cy", 1)), HALO)
-    ext_force = membrane(ext_pos, analysis, stiffness, synthesis)
+    packed = jnp.concatenate([wall_pos, wall_normal, density, wall_weight[:, None, :]], axis=1)
+    ext_pos, ext_wall = halos(cell_pos, packed, lax.axis_size("cx"), lax.axis_size("cy"))
     flat_pos = ext_pos.reshape(-1, 3, points)
-    flat_force = ext_force.reshape(-1, 3, points)
+    flat_force = membrane(flat_pos, analysis, stiffness, synthesis)
     count = row_count * col_count
     near_slots = slot(cell_near).reshape(count, -1)
     ids = jnp.arange(count, dtype=jnp.int32)
@@ -387,8 +457,6 @@
     step = 1.0 / (top + 1e-06)
     moved_cells = cell_pos + step * velocity.reshape(cell_pos.shape)
     patch_count = wall_pos.shape[0]
-    packed = jnp.concatenate([wall_pos, wall_normal, density, wall_weight[:, None, :]], axis=1)
-    ext_wall = with_halo(packed, ((("cx", "cy"), 0),), patch_count)
     all_patches = patch_count * lax.axis_size(("cx", "cy"))
     block_start = lax.axis_index(("cx", "cy")) * patch_count
     own_patches = jnp.arange(patch_count, dtype=jnp.int32) + patch_count

time: 126 us -> 120 us (0.952)
  Pallas kernels: 68.2 us -> 104 us
  starting transfers between devices: 13 us -> 0 us
  local copies, waits for them, and re-layouts: 21.3 us -> 8.81 us
  waiting for transfers between devices: 6.96 us -> 0 us
  other arithmetic: 9.83 us -> 5.1 us
  matrix products: 4.15 us -> 0 us
    pallas_call x0 -> x2, Pallas kernels: none -> 35 us  [the longest x1 29.1 us: halos(): pl.pallas_call(functools.partial(halo_kernel, size_x, size_y), out_shape=...]
    ppermute x6 -> x0, starting transfers between devices: 13 us -> none  [the longest x3 12.4 us: with_halo(): after = lax.ppermute(initial, axis, down)]
    ppermute x6 -> x0, waiting for transfers between devices: 6.96 us -> none  [the longest x3 6.95 us: with_halo(): before = lax.ppermute(last, axis, up)]
    concatenate x3 -> x0, local copies, waits for them, and re-layouts: 4.43 us -> none  [with_halo(): value = jnp.concatenate([before, value, after], axis=dim)]
    dot_general x1 -> x0, matrix products: 4.15 us -> none  [membrane(): force = -jnp.dot(scaled, synthesis, preferred_element_type=jnp.float32)]
    another operation x1 -> x0, local copies, waits for them, and re-layouts: 2.92 us -> none  [body(): flat_force = ext_force.reshape(-1, 3, points)]
    div x2 -> x0, local copies, waits for them, and re-layouts: 2.56 us -> none  [membrane(): centred = positions - jnp.mean(positions, axis=-1, keepdims=True)]
    reduce_sum x1 -> x0, other arithmetic: 2.26 us -> none  [membrane(): centred = positions - jnp.mean(positions, axis=-1, keepdims=True)]
  transfers between devices with their start and end apart: 6 -> 0, of which waited for: 2 -> 0; matrix products, arithmetic and copies ran while one was open for 9% -> 0% of each run, Pallas kernels for 0% -> 0%
where the time goes in v3:
time: 120 us
  Pallas kernels  104 us (87%)
  local copies, waits for them, and re-layouts  8.81 us (7%)
  other arithmetic  5.1 us (4%)
  between operations  1.4 us (1%)
    pallas_call x1, Pallas kernels, cell_velocity(): pl.pallas_call(functools.partial(cell_kernel, near=near), grid_spec=pltpu...  40.5 us
    pallas_call x1, Pallas kernels, halos(): pl.pallas_call(functools.partial(halo_kernel, size_x, size_y), out_shape=...  29.1 us
    pallas_call x1, Pallas kernels, wall_density(): pl.pallas_call(functools.partial(wall_kernel, near=near, listed=listed),...  17.6 us
    pallas_call x1, Pallas kernels, top_of_all(): pl.pallas_call(functools.partial(top_kernel, size_x, size_y), out_shape=j...  11.2 us
    unnamed x13, local copies, waits for them, and re-layouts  6.16 us
    pallas_call x1, Pallas kernels, membrane(): pl.pallas_call(membrane_kernel, out_shape=jax.ShapeDtypeStruct(positions....  5.93 us

profile of v3, /device:TPU:0, one launch (start us, length us, event | category | flops | bytes accessed | tf_op | source)
XLA Modules:
  0.0 119.6 jit_solution(3476579996356549061)
XLA Ops:
  0.6 1.2 %reshape.32.drag_ref = f32[16]{0:T(128)} reshape(f32[4,4]{1,0:T(4,128)} %param.13) | data formatting | bytes 128 | tf_op jit(solution)/shard_map/reshape | solution.py:450
  1.9 0.5 fusion.16.own_ref
  2.4 0.7 fusion
  3.1 0.7 copy.29
  3.9 0.8 copy.26
  4.6 0.8 copy.22
  5.4 0.6 fusion.5.cell_slot_ref
  6.0 0.7 pad_add_fusion.patch_slot_ref
  6.7 0.7 broadcast_in_dim.7
  7.4 0.8 copy.16.target_ref
  8.1 0.0 copy-start.1
  8.1 0.8 copy.17
  8.9 0.8 copy.18
  9.7 0.7 pad_maximum_fusion.wall_ref
  10.4 1.8 %copy.15.cell_ref = f32[4,4,3,1024]{3,2,1,0:T(4,128)} copy(f32[4,4,3,1024]{3,1,2,0:T(4,128)} %param.12) | data formatting | bytes 393216 | tf_op args[0]
  12.1 29.1 %halos.1 = (f32[10,10,3,1024]{3,2,1,0:T(4,128)}, f32[24,10,256]{2,1,0:T(8,128)}) custom-call(f32[4,4,3,1024]{3,2,1,0:T(4,128)} %copy.15.cell_ref, f32[8,10,256]{2,1,0:T(8,128)} %pad_maximum_fusion.wall_ref), custom_call_target="tpu_custom_call" | custom-call | tf_op jit(solution)/shard_map/halos/pallas_call | solution.py:77
  41.2 5.9 %membrane.1.force_ref = f32[100,3,1024]{2,1,0:T(4,128)} custom-call(f32[100,3,1024]{2,1,0:T(4,128)} %bitcast.7, bf16[1024,1024]{1,0:T(8,128)(2,1)} %analysis_ref.1, f32[1,1024]{1,0:T(1,128)} %bitcast.13, bf16[1024,1024]{1,0:T(8,128)(2,1)} %synthesis_ref.1), custom_call_target="tpu_custom_call" | custom-call | tf_op jit(solution)/shard_map/membrane/pallas_call | solution.py:106
  47.2 17.6 %wall_density.1 = f32[8,3,256]{2,1,0:T(4,128)} custom-call(s32[8,2]{1,0:T(8,128)} %fusion.5.cell_slot_ref, s32[8,5]{1,0:T(8,128)} %pad_add_fusion.patch_slot_ref, f32[8,3,256]{2,1,0:T(4,128)} %copy-done.1, f32[100,3,1024]{2,1,0:T(4,128)} %bitcast.8, f32[100,3,1024]{2,1,0:T(4,128)} %membrane.1.force_ref, f32[24,10,256]{2,1,0:T(8,128)} %get-tuple-element.9.wall_ref), custom_call_target="tpu_custom_call" | custom-call | tf_op jit(solution)/shard_map/wall_density/pallas_call | solution.py:322
  64.8 40.5 %cell_velocity.1 = (f32[16,3,1024]{2,1,0:T(4,128)}, f32[1,128]{1,0:T(1,128)}) custom-call(s32[16,2]{1,0:T(8,128)} %bitcast.12, s32[16]{0:T(128)} %fusion.16.own_ref, f32[16]{0:T(128)} %reshape.32.drag_ref, f32[16,3,1024]{2,1,0:T(4,128)} %bitcast.10, f32[100,3,1024]{2,1,0:T(4,128)} %bitcast.9, f32[100,3,1024]{2,1,0:T(4,128)} %membrane.1.force_ref), custom_call_target="tpu_custom_call" | custom-call | tf_op jit(solution)/shard_map/cell_velocity/pallas_call | solution.py:249
  105.3 0.0 copy-done.2
  105.3 0.6 copy.28
  105.9 11.2 %top_of_all.1 = f32[1,128]{1,0:T(1,128)} custom-call(f32[1,128]{1,0:T(1,128)} %get-tuple-element.7.mine_ref), custom_call_target="tpu_custom_call" | custom-call | tf_op jit(solution)/shard_map/top_of_all/pallas_call | solution.py:391
  117.8 1.0 broadcast_multiply_fusion
  118.8 0.8 copy_add_fusion
  (6 shorter events, 0.0 us)
Async XLA Ops:
  8.1 39.0 %copy-start.1 = (f32[8,3,256]{2,1,0:T(4,128)}, f32[8,3,256]{2,1,0:T(4,128)S(1)}, u32[]{:S(2)}) copy-start(f32[8,3,256]{2,1,0:T(4,128)S(1)} %copy.16.target_ref) | copy-start | bytes 73732
  64.8 40.5 %copy-start.2 = (f32[8,3,256]{2,1,0:T(4,128)S(1)}, f32[8,3,256]{2,1,0:T(4,128)}, u32[]{:S(2)}) copy-start(f32[8,3,256]{2,1,0:T(4,128)} %wall_density.1) | copy-start | bytes 73732
  64.8 54.0 %copy-start = (f32[4,4,3,1024]{3,1,2,0:T(4,128)S(1)}, f32[4,4,3,1024]{3,1,2,0:T(4,128)}, u32[]{:S(2)}) copy-start(f32[4,4,3,1024]{3,1,2,0:T(4,128)} %param.12) | copy-start | bytes 589828
